TPU v7x, 32 devices: a whole 2x2x4 slice. The times are simulated.
32 devices in a mesh: segment: 2 (over core), clip: 4 (over z), tile: 4 (over y, x).
Axes of the slice: x: 2, y: 2, z: 4, core: 2. Of those that a mesh axis runs over, the one named last changes fastest.
Arguments:
- video: bfloat16 [4, 4, 3, 12, 4, 256], P('clip', 'tile'), may hold values from -6 to 6
- cotangent: bfloat16 [4, 4, 3, 12, 4, 256], P('clip', 'tile'), may hold values from -6 to 6
- weights: bfloat16 [2, 27, 256, 256], P('segment'), may hold values from -0.078125 to 0.078125
- neighbours: int32 [4, 4, 2], P('clip', 'tile'), may hold values from 0 to 4, as said below
- rows_used: int32 [4, 4], P('clip', 'tile'), may hold values from 3 to 12, as said below
- cols_used: int32 [4], P('clip'), may hold values from 2 to 4, as said below
Outputs:
- section_out: bfloat16 [2, 4, 4, 3, 12, 4, 256], P('segment', 'clip', 'tile')
- grads: float32 [2, 3, 589824], P('segment', None, ('clip', 'tile'))
Inputs may be any that keep to these rules, and one draw needn't show every extreme that they name: `neighbours`: in each clip the strips of its frames lie on the 4 tiles in an order of their own: entry 0 names the tile of the strip above, entry 1 the tile of the strip below, 4 where there is none; exactly one strip of each clip has none above and one has none below, and the entries chain all 4 strips of a clip top to bottom. `rows_used`: in every clip some strip has 12 rows. `cols_used`: some clip has 4 columns.
All inputs are finite; a program needn't handle non-finite values.
Results may differ from a plain program's by a relative error of at most 0.0054.
Values may be sent and summed in bfloat16 or wider, within the bound.
A program may use at most 576 MiB of HBM per device.

v0:
```python
import jax
import jax.numpy as jnp
from jax import lax
from jax.sharding import PartitionSpec as P


def shifted(block, axis, distance):
    devices = range(lax.axis_size(axis))
    route = [(i - distance, i) for i in devices if i - distance in devices]
    return lax.ppermute(block, axis, route)


def silu_grad(values):
    sigmoid = jax.nn.sigmoid(values)
    return sigmoid * (1.0 + values * (1.0 - sigmoid))


def pad_block(strip_field, upper, bottom, row_count):
    frame_count, height, columns, channels = strip_field.shape
    blank = jnp.zeros((frame_count, 1, columns, channels), strip_field.dtype)
    padded = jnp.concatenate([upper[:, None], strip_field, blank], axis=1)
    padded = lax.dynamic_update_slice_in_dim(padded, bottom[:, None], row_count + 1, axis=1)
    return jnp.pad(padded, ((0, 0), (0, 0), (1, 1), (0, 0)))


def patches(stacked, frame_count, height, columns):
    pieces = []
    for depth_off in range(3):
        for row_off in range(3):
            for col_off in range(3):
                pieces.append(
                    stacked[
                        depth_off : depth_off + frame_count,
                        row_off : row_off + height,
                        col_off : col_off + columns,
                    ]
                )
    return jnp.concatenate(pieces, axis=-1).reshape(frame_count * height * columns, -1)


def every_tap_entries(patch_fwd, weighting, start, count, channels):
    span = 9 * channels
    row_total = min(count // channels + 2, span)
    row_low = jnp.minimum(start // channels, span - row_total)
    columns = jnp.concatenate(
        [
            lax.dynamic_slice_in_dim(patch_fwd, tap * span + row_low, row_total, 1)
            for tap in range(3)
        ],
        axis=1,
    )
    contract = (((0,), (0,)), ((), ()))
    block = lax.dot_general(
        columns, weighting, contract, preferred_element_type=jnp.float32
    ).reshape(3, -1)
    return block.T


def local(video, cotangent, weights, neighbours, rows_used, cols_used):
    window = video[0, 0]
    frame_count, height, columns, channels = window.shape
    tile_count = lax.axis_size("tile")
    section = lax.axis_index("segment")
    row_count = rows_used[0, 0]
    col_count = cols_used[0]
    upper_tile = neighbours[0, 0, 0]
    lower_tile = neighbours[0, 0, 1]
    row_ids = jnp.arange(height, dtype=jnp.int32)
    col_ids = jnp.arange(columns, dtype=jnp.int32)
    inside = (row_ids[:, None] < row_count) & (col_ids[None, :] < col_count)
    inside_mask = inside[None, :, :, None]
    kernel = weights[0]
    forward_mat = kernel.reshape(27 * channels, channels)
    backward_mat = kernel[::-1].transpose(0, 2, 1).reshape(27 * channels, channels)
    front_zero = jnp.zeros((2, height + 2, columns + 2, channels), jnp.bfloat16)

    def halo_block(field):
        leading = field[:, 0]
        trailing = lax.dynamic_index_in_dim(field, row_count - 1, axis=1, keepdims=False)
        both_rows = jnp.stack([leading, trailing], axis=1)
        gathered = lax.all_gather(both_rows[None], "tile", axis=0, tiled=True)
        upper = gathered[jnp.minimum(upper_tile, tile_count - 1), :, 1]
        bottom = gathered[jnp.minimum(lower_tile, tile_count - 1), :, 0]
        upper = jnp.where(upper_tile < tile_count, upper, jnp.zeros_like(upper))
        bottom = jnp.where(lower_tile < tile_count, bottom, jnp.zeros_like(bottom))
        return pad_block(field, upper, bottom, row_count)

    def advance(entry, history):
        count = entry.shape[0]
        activated = jax.nn.silu(entry.astype(jnp.float32)).astype(jnp.bfloat16)
        padded = halo_block(activated)
        stacked = jnp.concatenate([history, padded], axis=0)
        mixed = jnp.dot(
            patches(stacked, count, height, columns),
            forward_mat,
            preferred_element_type=jnp.float32,
        ).reshape(entry.shape)
        result = jnp.where(inside_mask, entry.astype(jnp.float32) + mixed, 0.0).astype(jnp.bfloat16)
        return (result, stacked[-2:], padded)

    source = jnp.where(inside_mask, window, jnp.zeros_like(window))
    is_encoder = section == 0
    first_out, first_hist, first_pad = advance(source, front_zero)
    latent = shifted(first_out, "segment", 1)
    second_out, second_hist, second_pad = advance(latent, front_zero)
    own_out = jnp.where(is_encoder, first_out, second_out)
    own_input = jnp.where(is_encoder, source, latent)
    own_pad = jnp.where(is_encoder, first_pad, second_pad)
    target = jnp.where(inside_mask, cotangent[0, 0], jnp.zeros_like(cotangent[0, 0]))
    patch_fwd = patches(
        jnp.concatenate([front_zero, own_pad], axis=0), frame_count, height, columns
    )
    back_stack = jnp.concatenate([halo_block(target), front_zero], axis=0)
    spread = jnp.dot(
        patches(back_stack, frame_count, height, columns),
        backward_mat,
        preferred_element_type=jnp.float32,
    ).reshape(target.shape)
    own_grad = jnp.where(
        inside_mask,
        target.astype(jnp.float32) + silu_grad(own_input.astype(jnp.float32)) * spread,
        0.0,
    ).astype(jnp.bfloat16)
    returned = shifted(own_grad, "segment", -1)
    weighting = jnp.where(is_encoder, returned, target).reshape(-1, channels)
    flat_rows = 9 * channels * channels // lax.axis_size(("clip", "tile"))
    shares = lax.psum_scatter(
        every_tap_entries(
            patch_fwd,
            weighting,
            jnp.int32(0),
            flat_rows * lax.axis_size(("clip", "tile")),
            channels,
        ),
        ("clip", "tile"),
        scatter_dimension=0,
        tiled=True,
    )
    summed = shares.T
    return (own_out[None, None, None], summed[None])


def solution(mesh):
    in_specs = (
        P("clip", "tile", None, None, None, None),
        P("clip", "tile", None, None, None, None),
        P("segment", None, None, None),
        P("clip", "tile", None),
        P("clip", "tile"),
        P("clip"),
    )
    out_specs = (
        P("segment", "clip", "tile", None, None, None, None),
        P("segment", None, ("clip", "tile")),
    )
    return jax.shard_map(local, mesh=mesh, in_specs=in_specs, out_specs=out_specs, check_vma=False)
```

profile of v0, /device:TPU:0, one launch (start us, length us, event | category | flops | bytes accessed | tf_op | source)
XLA Modules:
  0.0 367.3 jit_solution(6660135488782941422)
XLA Ops:
  7.2 0.0 all-reduce.10.cloned.1.call-start
  7.2 1.3 fusion.28
  12.4 0.1 broadcast_and_fusion
  12.5 1.0 bitcast_select_fusion
  13.5 1.0 fusion.18
  14.6 9.7 %all-gather.2 = bf16[12,2,4,256]{3,2,1,0:T(4,128)(2,1)S(1)} all-gather(bf16[3,2,4,256]{3,2,1,0:T(4,128)(2,1)S(1)} %copy.127), channel_id=4, replica_groups=mesh['segment'=2,'clip'=4,'tile'=4] {'tile'}, dimensions={0}, use_global_device_ids=true | all-gather | bytes 61440 | tf_op jit(solution)/shard_map/all_gather | solution.py:81
  24.4 8.2 %all-gather = bf16[12,2,4,256]{3,2,1,0:T(4,128)(2,1)S(1)} all-gather(bf16[3,2,4,256]{3,2,1,0:T(4,128)(2,1)S(1)} %copy.120), channel_id=2, replica_groups=mesh['segment'=2,'clip'=4,'tile'=4] {'tile'}, dimensions={0}, use_global_device_ids=true | all-gather | bytes 61440 | tf_op jit(solution)/shard_map/all_gather | solution.py:81
  32.7 0.1 pad.29.clone
  32.8 0.1 maximum_maximum_fusion.2
  32.9 0.1 dynamic_update_slice.9
  33.0 0.0 copy-start
  33.1 0.0 copy-start.2
  33.7 1.4 copy-done
  35.0 0.0 copy-done.2
  35.0 0.9 fusion.2
  35.9 1.3 collective-permute-start
  37.2 0.1 dynamic_update_slice.11
  37.4 5.7 %copy.130 = bf16[1,27,256,256]{2,3,1,0:T(8,128)(2,1)} copy(bf16[1,27,256,256]{3,2,1,0:T(8,128)(2,1)} %param.8) | data formatting | bytes 7077888 | tf_op args[2]
  43.7 0.0 copy-start.3
  43.7 4.2 %rev.3 = bf16[27,256,256]{1,2,0:T(8,128)(2,1)} reverse(bf16[27,256,256]{1,2,0:T(8,128)(2,1)} %bitcast.80), dimensions={0} | reverse | bytes 7077888 | tf_op jit(solution)/shard_map/rev | solution.py:74
  47.9 0.0 collective-permute-done
  48.0 0.0 copy-done.3
  48.0 3.0 fusion.14
  51.0 7.3 %all-gather.1 = bf16[12,2,4,256]{3,2,1,0:T(4,128)(2,1)S(1)} all-gather(bf16[3,2,4,256]{3,2,1,0:T(4,128)(2,1)S(1)} %copy.123), channel_id=3, replica_groups=mesh['segment'=2,'clip'=4,'tile'=4] {'tile'}, dimensions={0}, use_global_device_ids=true | all-gather | bytes 61440 | tf_op jit(solution)/shard_map/all_gather | solution.py:81
  58.3 0.1 maximum_maximum_fusion.1
  58.4 0.1 dynamic_update_slice.10
  59.2 1.5 collective-permute-start.1
  60.7 1.7 collective-permute-done.1
  62.4 4.0 %convolution_bitcast_fusion = f32[6912,256]{1,0:T(8,128)} fusion(bf16[3,12,4,6912]{3,1,2,0:T(8,128)(2,1)S(1)} %constant_dynamic-update-slice_fusion.54, bf16[3,12,4,256]{3,1,2,0:T(8,128)(2,1)S(1)} %collective-permute-done.1, pred[]{:T(512)S(6)} %eq.3, bf16[1,1,3,12,4,256]{5,4,3,2,1,0:T(4,128)(2,1)S(1)} %copy-done.3, pred[12,4]{0,1:T(4,128)(4,1)S(1)} %broadcast_and_fusion), kind=kOutput, calls=%fused_computation | convolution fusion | flops 509681664 | bytes 9216049 | tf_op jit(solution)/shard_map/dot_general | solution.py:53
  66.4 10.6 %reshape.152 = f32[3,589824]{1,0:T(4,128)} reshape(f32[6912,256]{1,0:T(8,128)} %convolution_bitcast_fusion) | data formatting | bytes 14155776 | tf_op jit(solution)/shard_map/reshape | solution.py:55
  77.0 0.0 copy-start.4
  77.0 0.0 all-reduce.10.cloned.1.call-update
  77.0 0.6 copy-done.4
  77.6 0.6 dynamic-slice
  78.9 0.0 copy-start.1
  79.5 1.4 copy-done.1
  80.9 0.9 fusion.5
  81.8 0.7 copy.131
  82.5 275.6 %all-reduce.10.cloned.1.call-done = f32[589824,3]{0,1:T(4,128)} async-done(((f32[589824,3]{0,1:T(4,128)}), f32[589824,3]{0,1:T(4,128)}) %all-reduce.10.cloned.1.call-update) | async-done | bytes 7077904
  358.1 1.2 dynamic-slice_bitcast_fusion
  359.2 1.2 copy.132
  (130 shorter events, 2.2 us)
Async XLA Ops:
  7.2 350.9 %all-reduce.10.cloned.1.call-start = ((), (), s32[]{:S(2)}) async-start(), calls=%async_computation | async-start | bytes 18874368
  33.0 2.0 copy-start
  33.1 2.0 copy-start.2
  35.9 12.0 %collective-permute-start = (bf16[3,12,4,256]{3,1,2,0:T(8,128)(2,1)S(1)}, bf16[3,12,4,256]{3,1,2,0:T(8,128)(2,1)S(1)}, u32[]{:S(2)}, u32[]{:S(2)}) collective-permute-start(bf16[3,12,4,256]{3,1,2,0:T(8,128)(2,1)S(1)} %fusion.2), channel_id=1, source_target_pairs={{0,16},{1,17},{2,18},{3,19},{4,20},{5,21},{6,22},{7,23},{8,24},{9,... | collective-permute-start | bytes 221192 | tf_op jit(solution)/shard_map/ppermute | solution.py:10
  43.7 4.2 %copy-start.3 = (bf16[1,1,3,12,4,256]{5,4,3,2,1,0:T(4,128)(2,1)S(1)}, bf16[1,1,3,12,4,256]{5,4,3,2,1,0:T(4,128)(2,1)}, u32[]{:S(2)}) copy-start(bf16[1,1,3,12,4,256]{5,4,3,2,1,0:T(4,128)(2,1)} %param.7) | copy-start | bytes 221188
  59.2 3.2 collective-permute-start.1
  77.0 0.7 copy-start.4
  78.9 2.0 copy-start.1
Sparse Core Ops, SparseCore 0:
  77.1 280.8 all-reduce.9
where the time goes:
time: 368 us; the launch traced here: 367 us
  waiting for transfers between devices  277 us (75%)
  local copies, waits for them, and re-layouts  31.2 us (8%)
  blocking collectives  25.2 us (7%)
  between operations  19.7 us (5%)
  matrix products  8.71 us (2%)
    unnamed x2, waiting for transfers between devices  276 us
    all_gather x3, blocking collectives, halo_block(): gathered = lax.all_gather(both_rows[None], 'tile', axis=0, tiled=True)  25.2 us
    unnamed x118, local copies, waits for them, and re-layouts  13.4 us
    reshape x1, local copies, waits for them, and re-layouts, every_tap_entries(): block = lax.dot_general(columns, weighting, contract, preferred_element_t...  10.6 us
  transfers between devices with their start and end apart: 3, of which 2 were waited for; matrix products, arithmetic and copies ran while one was open for 4% of the time, Pallas kernels for 0%

commit v1 on v0

--- a/solution.py
+++ b/solution.py
@@ -38,22 +38,42 @@
     return jnp.concatenate(pieces, axis=-1).reshape(frame_count * height * columns, -1)
 
 
-def every_tap_entries(patch_fwd, weighting, start, count, channels):
-    span = 9 * channels
-    row_total = min(count // channels + 2, span)
-    row_low = jnp.minimum(start // channels, span - row_total)
-    columns = jnp.concatenate(
+def own_entries(padded, weighting, axes):
+    frame_count, tall, columns, channels = padded.shape
+    height = tall - 2
+    payload = jnp.concatenate([padded.reshape(-1, channels), weighting], axis=0)
+    gathered = lax.all_gather(payload, axes, axis=0)
+    cut = frame_count * tall * columns
+    strips = gathered[:, :cut].reshape(-1, frame_count, tall, columns, channels)
+    strips = jnp.pad(strips, ((0, 0), (2, 0), (0, 0), (1, 1), (0, 0)))
+    upstream = gathered[:, cut:].reshape(-1, channels)
+    row_total = 9 * channels // lax.axis_size(axes)
+    start = lax.axis_index(axes) * row_total
+    low = jnp.minimum(start // channels, 8)
+    lower = []
+    for step in range(-(-row_total // channels) + 1):
+        tap = jnp.minimum(low + step, 8)
+        lower.append(
+            lax.dynamic_slice(
+                strips,
+                (0, 0, tap // 3, tap % 3, 0),
+                (strips.shape[0], frame_count + 2, height, columns, channels),
+            )
+        )
+    window = jnp.concatenate(lower, axis=-1)
+    window = lax.dynamic_slice_in_dim(window, start - low * channels, row_total, 4)
+    contract = (((0,), (0,)), ((), ()))
+    return jnp.stack(
         [
-            lax.dynamic_slice_in_dim(patch_fwd, tap * span + row_low, row_total, 1)
+            lax.dot_general(
+                window[:, tap : tap + frame_count].reshape(-1, row_total),
+                upstream,
+                contract,
+                preferred_element_type=jnp.float32,
+            ).reshape(-1)
             for tap in range(3)
-        ],
-        axis=1,
+        ]
     )
-    contract = (((0,), (0,)), ((), ()))
-    block = lax.dot_general(
-        columns, weighting, contract, preferred_element_type=jnp.float32
-    ).reshape(3, -1)
-    return block.T
 
 
 def local(video, cotangent, weights, neighbours, rows_used, cols_used):
@@ -107,9 +127,6 @@
     own_input = jnp.where(is_encoder, source, latent)
     own_pad = jnp.where(is_encoder, first_pad, second_pad)
     target = jnp.where(inside_mask, cotangent[0, 0], jnp.zeros_like(cotangent[0, 0]))
-    patch_fwd = patches(
-        jnp.concatenate([front_zero, own_pad], axis=0), frame_count, height, columns
-    )
     back_stack = jnp.concatenate([halo_block(target), front_zero], axis=0)
     spread = jnp.dot(
         patches(back_stack, frame_count, height, columns),
@@ -123,20 +140,7 @@
     ).astype(jnp.bfloat16)
     returned = shifted(own_grad, "segment", -1)
     weighting = jnp.where(is_encoder, returned, target).reshape(-1, channels)
-    flat_rows = 9 * channels * channels // lax.axis_size(("clip", "tile"))
-    shares = lax.psum_scatter(
-        every_tap_entries(
-            patch_fwd,
-            weighting,
-            jnp.int32(0),
-            flat_rows * lax.axis_size(("clip", "tile")),
-            channels,
-        ),
-        ("clip", "tile"),
-        scatter_dimension=0,
-        tiled=True,
-    )
-    summed = shares.T
+    summed = own_entries(own_pad[:, :, 1:-1], weighting, ("clip", "tile"))
     return (own_out[None, None, None], summed[None])
 
 

time: 368 us -> 163 us (0.44)
  waiting for transfers between devices: 277 us -> 61.8 us
  local copies, waits for them, and re-layouts: 31.2 us -> 37.7 us
  other arithmetic: 2.43 us -> 7.39 us
    unnamed x2 -> x1, waiting for transfers between devices: 276 us -> 0.02 us
    all_gather x0 -> x1, waiting for transfers between devices: none -> 60.1 us  [own_entries(): gathered = lax.all_gather(payload, axes, axis=0)]
    slice x0 -> x4, local copies, waits for them, and re-layouts: none -> 6 us  [the longest x1 2.51 us: own_entries(): strips = gathered[:, :cut].reshape(-1, frame_count, tall, columns, channels)]
    concatenate x0 -> x2, other arithmetic: none -> 4.5 us  [the longest x1 3.82 us: own_entries(): window = jnp.concatenate(lower, axis=-1)]
    reshape x1 -> x6, local copies, waits for them, and re-layouts: 10.6 us -> 8.4 us  [the longest x3 5.48 us: own_entries(): window[:, tap:tap + frame_count].reshape(-1, row_total)]
    unnamed x118 -> x95, local copies, waits for them, and re-layouts: 13.4 us -> 12.6 us
  transfers between devices with their start and end apart: 3 -> 3, of which waited for: 2 -> 2; matrix products, arithmetic and copies ran while one was open for 4% -> 8% of each run, Pallas kernels for 0% -> 0%
where the time goes in v1:
time: 163 us; the launch traced here: 162 us
  waiting for transfers between devices  61.8 us (38%)
  local copies, waits for them, and re-layouts  37.7 us (23%)
  blocking collectives  25.2 us (15%)
  between operations  19.1 us (12%)
  matrix products  8.63 us (5%)
  other arithmetic  7.39 us (5%)
  starting transfers between devices  2.62 us (2%)
    all_gather x1, waiting for transfers between devices, own_entries(): gathered = lax.all_gather(payload, axes, axis=0)  60.1 us
    all_gather x3, blocking collectives, halo_block(): gathered = lax.all_gather(both_rows[None], 'tile', axis=0, tiled=True)  25.2 us
    unnamed x95, local copies, waits for them, and re-layouts  12.6 us
    reshape x3, local copies, waits for them, and re-layouts, own_entries(): window[:, tap:tap + frame_count].reshape(-1, row_total)  5.48 us
    rev x1, local copies, waits for them, and re-layouts, local(): kernel[::-1].transpose(0, 2, 1).reshape(27 * channels, channels)  4.22 us
    dot_general x3, matrix products, own_entries(): lax.dot_general(window[:, tap:tap + frame_count].reshape(-1, row_total),...  3.94 us
    concatenate x1, other arithmetic, own_entries(): window = jnp.concatenate(lower, axis=-1)  3.82 us
    dynamic_slice x1, local copies, waits for them, and re-layouts, own_entries(): lax.dynamic_slice(strips, (0, 0, tap // 3, tap % 3, 0), (strips.shape[0],...  3.48 us
  transfers between devices with their start and end apart: 3, of which 2 were waited for; matrix products, arithmetic and copies ran while one was open for 8% of the time, Pallas kernels for 0%

profile of v1, /device:TPU:0, one launch (start us, length us, event | category | flops | bytes accessed | tf_op | source)
XLA Modules:
  0.0 162.4 jit_solution(4665979440617564632)
XLA Ops:
  7.2 0.0 all-gather.6.cloned.1.call-start
  7.2 1.3 fusion.28
  12.4 0.1 broadcast_and_fusion
  12.5 1.0 bitcast_select_fusion
  13.5 1.0 fusion.19
  14.6 9.7 %all-gather = bf16[12,2,4,256]{3,2,1,0:T(4,128)(2,1)S(1)} all-gather(bf16[3,2,4,256]{3,2,1,0:T(4,128)(2,1)S(1)} %copy.132), channel_id=2, replica_groups=mesh['segment'=2,'clip'=4,'tile'=4] {'tile'}, dimensions={0}, use_global_device_ids=true | all-gather | bytes 61440 | tf_op jit(solution)/shard_map/all_gather | solution.py:101
  24.4 8.2 %all-gather.2 = bf16[12,2,4,256]{3,2,1,0:T(4,128)(2,1)S(1)} all-gather(bf16[3,2,4,256]{3,2,1,0:T(4,128)(2,1)S(1)} %copy.140), channel_id=4, replica_groups=mesh['segment'=2,'clip'=4,'tile'=4] {'tile'}, dimensions={0}, use_global_device_ids=true | all-gather | bytes 61440 | tf_op jit(solution)/shard_map/all_gather | solution.py:101
  32.7 0.1 pad.40.clone
  32.8 0.1 maximum_maximum_fusion.2
  32.9 0.1 dynamic_update_slice.9
  33.7 1.4 copy-done
  35.0 0.9 fusion.3
  35.9 1.3 collective-permute-start
  37.2 0.1 dynamic_update_slice.11
  37.3 5.8 %copy.143 = bf16[1,27,256,256]{2,3,1,0:T(8,128)(2,1)} copy(bf16[1,27,256,256]{3,2,1,0:T(8,128)(2,1)} %param.8) | data formatting | bytes 7077888 | tf_op args[2]
  43.7 4.2 %rev.3 = bf16[27,256,256]{1,2,0:T(8,128)(2,1)} reverse(bf16[27,256,256]{1,2,0:T(8,128)(2,1)} %bitcast.88), dimensions={0} | reverse | bytes 7077888 | tf_op jit(solution)/shard_map/rev | solution.py:94
  48.0 3.0 %fusion.15 = (bf16[3,12,4,256]{3,1,2,0:T(8,128)(2,1)S(1)}, bf16[3,12,4,256]{3,1,2,0:T(8,128)(2,1)S(1)}) fusion(bf16[3,12,4,256]{3,1,2,0:T(8,128)(2,1)S(1)} %collective-permute-done, pred[12,4]{0,1:T(4,128)(4,1)S(1)} %broadcast_and_fusion, pred[]{:T(512)S(6)} %eq.6, bf16[1,1,3,12,4,256]{5,4,3,2,1,0:T(4,128)(2,1)S(1)} %copy-done.5, ...), kind=kOutput, calls=%fused_computation.85 | convolution fusion | flops 510418944 | bytes 5898289 | tf_op jit(solution)/shard_map/dot_general | solution.py:131
  51.0 7.3 %all-gather.1 = bf16[12,2,4,256]{3,2,1,0:T(4,128)(2,1)S(1)} all-gather(bf16[3,2,4,256]{3,2,1,0:T(4,128)(2,1)S(1)} %copy.135), channel_id=3, replica_groups=mesh['segment'=2,'clip'=4,'tile'=4] {'tile'}, dimensions={0}, use_global_device_ids=true | all-gather | bytes 61440 | tf_op jit(solution)/shard_map/all_gather | solution.py:101
  58.4 0.1 maximum_maximum_fusion.1
  58.5 1.3 collective-permute-start.1
  59.8 0.1 dynamic_update_slice.10
  59.9 1.7 %collective-permute-done.1 = bf16[3,12,4,256]{3,1,2,0:T(8,128)(2,1)S(1)} collective-permute-done((bf16[3,12,4,256]{3,1,2,0:T(8,128)(2,1)S(1)}, bf16[3,12,4,256]{3,1,2,0:T(8,128)(2,1)S(1)}, u32[]{:S(2)}, u32[]{:S(2)}) %collective-permute-start.1) | collective-permute-done | bytes 73760 | tf_op jit(solution)/shard_map/ppermute | solution.py:10
  61.7 0.1 broadcast_select_fusion
  61.8 0.7 pad_maximum_fusion.1
  62.5 0.0 all-gather.6.cloned.1.call-update
  63.3 1.4 copy-done.1
  64.7 0.9 fusion.6
  65.6 0.7 copy.145
  66.3 60.1 %all-gather.6.cloned.1.call-done = bf16[4992,256]{1,0:T(8,128)(2,1)} async-done(((bf16[312,256]{1,0:T(8,128)(2,1)}), bf16[4992,256]{1,0:T(8,128)(2,1)}) %all-gather.6.cloned.1.call-update) | async-done | bytes 2555920 | tf_op jit(solution)/shard_map/all_gather | solution.py:45
  126.4 2.5 %slice.389 = bf16[16,168,256]{2,1,0:T(8,128)(2,1)} slice(bf16[16,312,256]{2,1,0:T(8,128)(2,1)} %bitcast.90), slice={[0:16], [0:168], [0:256]} | slice | bytes 2752512 | tf_op jit(solution)/shard_map/slice | solution.py:47
  128.9 1.3 slice.391
  130.2 2.9 %reshape.170 = bf16[16,3,14,4,256]{4,3,2,1,0:T(4,128)(2,1)S(1)} reshape(bf16[16,168,256]{2,1,0:T(8,128)(2,1)} %slice.389) | data formatting | bytes 2752512 | tf_op jit(solution)/shard_map/reshape | solution.py:47
  133.1 3.5 %pad_dynamic-slice_fusion = (bf16[16,5,12,4,256]{4,3,2,1,0:T(4,128)(2,1)S(1)}, bf16[16,5,12,4,256]{4,3,2,1,0:T(4,128)(2,1)S(1)}) fusion(s32[]{:T(128)S(6)} %select_n.223, s32[]{:T(128)S(6)} %select_n.225, bf16[16,3,14,4,256]{4,3,2,1,0:T(4,128)(2,1)S(1)} %reshape.170, s32[]{:T(128)S(6)} %select_n.219, s32[]{:T(128)S(6)} %select_n.221), kind=kLoop, calls=%fused_computation | loop fusion | bytes 5308432 | tf_op jit(solution)/shard_map/dynamic_slice | solution.py:57
  136.6 3.8 %fusion = bf16[16,5,12,4,144]{4,3,2,1,0:T(4,128)(2,1)S(1)} fusion(s32[]{:T(128)S(6)} %select_n.226, bf16[16,5,12,4,256]{4,3,2,1,0:T(4,128)(2,1)S(1)} %get-tuple-element.22, bf16[16,5,12,4,256]{4,3,2,1,0:T(4,128)(2,1)S(1)} %get-tuple-element.21), kind=kLoop, calls=%fused_computation.4 | loop fusion | flops 2211840 | bytes 5038084 | tf_op jit(solution)/shard_map/concatenate | solution.py:63
  140.4 2.1 %fusion.24 = (bf16[16,3,12,4,144]{4,3,2,1,0:T(4,128)(2,1)}, bf16[16,3,12,4,144]{4,3,2,1,0:T(4,128)(2,1)S(1)}, bf16[16,3,12,4,144]{4,3,2,1,0:T(4,128)(2,1)S(1)}) fusion(bf16[16,5,12,4,144]{4,3,2,1,0:T(4,128)(2,1)S(1)} %fusion), kind=kLoop, calls=%fused_computation.198 | loop fusion | bytes 3981312 | tf_op jit(solution)/shard_map/slice | solution.py:69
  142.5 3.2 %reshape.171 = bf16[2304,144]{1,0:T(8,128)(2,1)} reshape(bf16[16,3,12,4,144]{4,3,2,1,0:T(4,128)(2,1)} %get-tuple-element.18) | data formatting | bytes 1327104 | tf_op jit(solution)/shard_map/reshape | solution.py:69
  145.7 1.7 %convolution_bitcast_fusion.2 = f32[1,1,144,256]{3,2,1,0:T(8,128)S(1)} fusion(bf16[2304,144]{1,0:T(8,128)(2,1)} %reshape.171, bf16[2304,256]{1,0:T(8,128)(2,1)S(1)} %bitcast.83), kind=kOutput, calls=%fused_computation.11 | convolution fusion | flops 169869312 | bytes 1990656 | tf_op jit(solution)/shard_map/dot_general | solution.py:68
  147.4 0.8 copy.148
  148.2 1.6 reshape.173
  149.8 1.7 %convolution_bitcast_fusion.1 = f32[1,1,144,256]{3,2,1,0:T(8,128)S(1)} fusion(bf16[2304,144]{1,0:T(8,128)(2,1)} %reshape.173, bf16[2304,256]{1,0:T(8,128)(2,1)S(1)} %bitcast.84), kind=kOutput, calls=%fused_computation.10 | convolution fusion | flops 169869312 | bytes 1990656 | tf_op jit(solution)/shard_map/dot_general | solution.py:68
  151.6 0.8 copy.149
  152.4 0.7 reshape.174
  153.1 0.5 convolution_bitcast_fusion
  153.6 0.2 copy.150
  153.8 0.3 copy-done.2
  154.0 0.1 copy-done.3
  154.1 0.4 pad_maximum_fusion
  154.5 1.1 broadcast_in_dim.60
  (117 shorter events, 1.9 us)
Async XLA Ops:
  7.2 119.2 %all-gather.6.cloned.1.call-start = ((), (), s32[]{:S(2)}) async-start(), calls=%async_computation | async-start | bytes 2715648 | tf_op jit(solution)/shard_map/all_gather | solution.py:45
  33.0 2.0 %copy-start = (bf16[1,27,256,256]{3,2,1,0:T(8,128)(2,1)S(1)}, bf16[1,27,256,256]{3,2,1,0:T(8,128)(2,1)}, u32[]{:S(2)}) copy-start(bf16[1,27,256,256]{3,2,1,0:T(8,128)(2,1)} %param.8) | copy-start | bytes 10616836
  33.0 2.0 %copy-start.5 = (bf16[1,1,3,12,4,256]{5,4,3,2,1,0:T(4,128)(2,1)S(1)}, bf16[1,1,3,12,4,256]{5,4,3,2,1,0:T(4,128)(2,1)}, u32[]{:S(2)}) copy-start(bf16[1,1,3,12,4,256]{5,4,3,2,1,0:T(4,128)(2,1)} %param.6) | copy-start | bytes 221188
  35.9 12.1 %collective-permute-start = (bf16[3,12,4,256]{3,1,2,0:T(8,128)(2,1)S(1)}, bf16[3,12,4,256]{3,1,2,0:T(8,128)(2,1)S(1)}, u32[]{:S(2)}, u32[]{:S(2)}) collective-permute-start(bf16[3,12,4,256]{3,1,2,0:T(8,128)(2,1)S(1)} %fusion.3), channel_id=1, source_target_pairs={{0,16},{1,17},{2,18},{3,19},{4,20},{5,21},{6,22},{7,23},{8,24},{9,... | collective-permute-start | bytes 221192 | tf_op jit(solution)/shard_map/ppermute | solution.py:10
  43.7 4.3 %copy-start.4 = (bf16[1,1,3,12,4,256]{5,4,3,2,1,0:T(4,128)(2,1)S(1)}, bf16[1,1,3,12,4,256]{5,4,3,2,1,0:T(4,128)(2,1)}, u32[]{:S(2)}) copy-start(bf16[1,1,3,12,4,256]{5,4,3,2,1,0:T(4,128)(2,1)} %param.7) | copy-start | bytes 221188
  58.5 3.2 %collective-permute-start.1 = (bf16[3,12,4,256]{3,1,2,0:T(8,128)(2,1)S(1)}, bf16[3,12,4,256]{3,1,2,0:T(8,128)(2,1)S(1)}, u32[]{:S(2)}, u32[]{:S(2)}) collective-permute-start(bf16[3,12,4,256]{3,1,2,0:T(8,128)(2,1)S(1)} %get-tuple-element.23), channel_id=1, source_target_pairs={{16,0},{17,1},{18,2},{19,3},{20,4},{21,5},{22,6},{23,7},{24,8},{25... | collective-permute-start | bytes 221192 | tf_op jit(solution)/shard_map/ppermute | solution.py:10
  62.7 2.0 %copy-start.1 = (bf16[1,27,256,256]{3,2,1,0:T(8,128)(2,1)S(1)}, bf16[1,27,256,256]{3,2,1,0:T(8,128)(2,1)}, u32[]{:S(2)}) copy-start(bf16[1,27,256,256]{3,2,1,0:T(8,128)(2,1)} %param.8) | copy-start | bytes 10616836
  153.1 0.9 copy-start.2
  153.1 1.0 copy-start.3
Sparse Core Ops, SparseCore 0:
  62.6 63.7 all-gather.5

commit v2 on v1

v2 whole, which is shorter than its diff:
```python
import jax
import jax.numpy as jnp
from jax import lax
from jax.experimental import pallas as pl
from jax.experimental.pallas import tpu as pltpu
from jax.sharding import PartitionSpec as P


def shifted(block, axis, distance):
    devices = range(lax.axis_size(axis))
    route = [(i - distance, i) for i in devices if i - distance in devices]
    return lax.ppermute(block, axis, route)


def silu_grad(values):
    sigmoid = jax.nn.sigmoid(values)
    return sigmoid * (1.0 + values * (1.0 - sigmoid))


def pad_block(strip_field, upper, bottom, row_count):
    frame_count, height, columns, channels = strip_field.shape
    blank = jnp.zeros((frame_count, 1, columns, channels), strip_field.dtype)
    padded = jnp.concatenate([upper[:, None], strip_field, blank], axis=1)
    padded = lax.dynamic_update_slice_in_dim(padded, bottom[:, None], row_count + 1, axis=1)
    return jnp.pad(padded, ((0, 0), (0, 0), (1, 1), (0, 0)))


def patches(stacked, frame_count, height, columns):
    pieces = []
    for depth_off in range(3):
        for row_off in range(3):
            for col_off in range(3):
                pieces.append(
                    stacked[
                        depth_off : depth_off + frame_count,
                        row_off : row_off + height,
                        col_off : col_off + columns,
                    ]
                )
    return jnp.concatenate(pieces, axis=-1).reshape(frame_count * height * columns, -1)


def back_kernel(patch_ref, weight_ref, out_ref):
    taps, channels = weight_ref.shape[0], weight_ref.shape[2]
    total = jnp.zeros(out_ref.shape, jnp.float32)
    for tap in range(taps):
        total += lax.dot_general(
            patch_ref[:, tap * channels : (tap + 1) * channels],
            weight_ref[taps - 1 - tap],
            (((1,), (1,)), ((), ())),
            preferred_element_type=jnp.float32,
        )
    out_ref[...] = total


def conv_back_dot(patch_mat, kernel):
    rows, channels = patch_mat.shape[0], kernel.shape[1]
    return pl.pallas_call(
        back_kernel,
        out_shape=jax.ShapeDtypeStruct((rows, channels), jnp.float32),
        in_specs=[pl.BlockSpec(memory_space=pltpu.VMEM)] * 2,
        out_specs=pl.BlockSpec(memory_space=pltpu.VMEM),
        compiler_params=pltpu.CompilerParams(vmem_limit_bytes=24 * 2**20),
    )(patch_mat, kernel)


def own_entries(acts, ups, axes, frame_count, height, columns):
    strips, channels = acts.shape[0], acts.shape[-1]
    tall = acts.shape[1] // frame_count
    acts = acts.reshape(strips, frame_count, tall, channels)
    ups = ups.reshape(strips, frame_count, height * columns, channels)
    row_total = 9 * channels // lax.axis_size(axes)
    start = lax.axis_index(axes) * row_total
    low = jnp.minimum(start // channels, 8)
    lead = 16
    ups = jnp.pad(ups, ((0, 0), (0, 0), (lead, lead + tall - height * columns), (0, 0)))
    column = lax.broadcasted_iota(jnp.int32, (1, 1, ups.shape[2], 1), 2) % columns
    per_tap = []
    for step in range(-(-row_total // channels) + 1):
        tap = jnp.minimum(low + step, 8)
        row_off, col_off = tap // 3, tap % 3
        beside = column + col_off - 1
        held = jnp.where((beside >= 0) & (beside < columns), ups, jnp.zeros_like(ups))
        moved = lax.dynamic_slice_in_dim(held, lead - (columns * row_off + col_off - 1), tall, 2)
        per_tap.append(moved)
    contract = (((0, 1, 2), (0, 1, 2)), ((), ()))
    by_frame = []
    for tap in range(3):
        count = frame_count - 2 + tap
        entries = jnp.concatenate(
            [
                lax.dot_general(
                    acts[:, :count],
                    moved[:, frame_count - count :],
                    contract,
                    preferred_element_type=jnp.float32,
                )
                for moved in per_tap
            ],
            axis=0,
        )
        by_frame.append(
            lax.dynamic_slice_in_dim(entries, start - low * channels, row_total, 0).reshape(-1)
        )
    return jnp.stack(by_frame)


def local(video, cotangent, weights, neighbours, rows_used, cols_used):
    frame_count, height, columns, channels = video.shape[2:]
    tile_count = lax.axis_size("tile")
    section = lax.axis_index("segment")
    row_count = rows_used[0, 0]
    col_count = cols_used[0]
    upper_tile = neighbours[0, 0, 0]
    lower_tile = neighbours[0, 0, 1]
    row_ids = jnp.arange(height, dtype=jnp.int32)
    col_ids = jnp.arange(columns, dtype=jnp.int32)
    inside = (row_ids[:, None] < row_count) & (col_ids[None, :] < col_count)
    inside_mask = inside[None, :, :, None]
    kernel = weights[0]
    forward_mat = kernel.reshape(27 * channels, channels)
    front_zero = jnp.zeros((2, height + 2, columns + 2, channels), jnp.bfloat16)

    def halo_block(field):
        leading = field[:, 0]
        trailing = lax.dynamic_index_in_dim(field, row_count - 1, axis=1, keepdims=False)
        both_rows = jnp.stack([leading, trailing], axis=1)
        gathered = lax.all_gather(both_rows[None], "tile", axis=0, tiled=True)
        upper = gathered[jnp.minimum(upper_tile, tile_count - 1), :, 1]
        bottom = gathered[jnp.minimum(lower_tile, tile_count - 1), :, 0]
        upper = jnp.where(upper_tile < tile_count, upper, jnp.zeros_like(upper))
        bottom = jnp.where(lower_tile < tile_count, bottom, jnp.zeros_like(bottom))
        return pad_block(field, upper, bottom, row_count)

    def front(padded):
        stacked = jnp.concatenate([front_zero, padded], axis=0)
        patch_mat = patches(stacked, frame_count, height, columns)
        return jnp.dot(patch_mat, forward_mat, preferred_element_type=jnp.float32)

    def back(padded):
        stacked = jnp.concatenate([padded, front_zero], axis=0)
        return conv_back_dot(patches(stacked, frame_count, height, columns), kernel)

    def flat(field):
        rows = field.reshape(-1, channels)
        return jnp.pad(rows, ((0, frame_count * (height + 2) * columns - rows.shape[0]), (0, 0)))

    axes = ("clip", "tile")
    is_encoder = section == 0
    source = jnp.where(inside_mask, video[0, 0], 0).astype(jnp.bfloat16)
    target = jnp.where(inside_mask, cotangent[0, 0], 0).astype(jnp.bfloat16)
    active = jax.nn.silu(source.astype(jnp.float32)).astype(jnp.bfloat16)
    padded = halo_block(jnp.where(is_encoder, active, target))
    early = jnp.where(is_encoder, flat(padded[:, :, 1:-1]), flat(target))
    early_all = lax.all_gather(early, axes, axis=0)
    mixed = lax.cond(is_encoder, front, back, padded).reshape(target.shape)
    hidden = jnp.where(inside_mask, source.astype(jnp.float32) + mixed, 0.0).astype(jnp.bfloat16)
    latent = shifted(hidden, "segment", 1)
    wide = latent.astype(jnp.float32)
    own_grad = jnp.where(
        inside_mask, target.astype(jnp.float32) + silu_grad(wide) * mixed, 0.0
    ).astype(jnp.bfloat16)
    returned = shifted(own_grad, "segment", -1)
    padded_two = halo_block(jax.nn.silu(wide).astype(jnp.bfloat16))
    late = jnp.where(is_encoder, flat(returned), flat(padded_two[:, :, 1:-1]))
    late_all = lax.all_gather(late, axes, axis=0)
    decoded = jnp.where(
        inside_mask, wide + front(padded_two).reshape(target.shape), 0.0
    ).astype(jnp.bfloat16)
    own_out = jnp.where(is_encoder, hidden, decoded)
    acts = jnp.where(is_encoder, early_all, late_all)
    ups = jnp.where(is_encoder, late_all, early_all)[:, : frame_count * height * columns]
    summed = own_entries(acts, ups, axes, frame_count, height, columns)
    return (own_out[None, None, None], summed[None])


def solution(mesh):
    in_specs = (
        P("clip", "tile", None, None, None, None),
        P("clip", "tile", None, None, None, None),
        P("segment", None, None, None),
        P("clip", "tile", None),
        P("clip", "tile"),
        P("clip"),
    )
    out_specs = (
        P("segment", "clip", "tile", None, None, None, None),
        P("segment", None, ("clip", "tile")),
    )
    return jax.shard_map(local, mesh=mesh, in_specs=in_specs, out_specs=out_specs, check_vma=False)
```

time: 163 us -> 158 us (0.969)
  local copies, waits for them, and re-layouts: 37.7 us -> 7.75 us
  starting transfers between devices: 2.62 us -> 23.1 us
  waiting for transfers between devices: 61.8 us -> 76.6 us
  blocking collectives: 25.2 us -> 17.9 us
  matrix products: 8.63 us -> 6.44 us
    ppermute x2, starting transfers between devices: 2.59 us -> 23 us  [shifted(): return lax.ppermute(block, axis, route)]
    all_gather x1 -> x2, waiting for transfers between devices: 60.1 us -> 74.4 us  [the longest x1 59.1 us: local(): late_all = lax.all_gather(late, axes, axis=0)]
    unnamed x95 -> x34, local copies, waits for them, and re-layouts: 12.6 us -> 1.57 us
    reshape x6 -> x3, local copies, waits for them, and re-layouts: 8.4 us -> 0.08 us  [flat(): rows = field.reshape(-1, channels)]
    all_gather x3 -> x2, blocking collectives: 25.2 us -> 17.9 us  [halo_block(): gathered = lax.all_gather(both_rows[None], 'tile', axis=0, tiled=True)]
    slice x4 -> x1, local copies, waits for them, and re-layouts: 6 us -> 0.08 us  [local(): jnp.where(is_encoder, late_all, early_all)]
    select_n x3 -> x6, other arithmetic: 1.07 us -> 5.74 us  [the longest x1 1.93 us: local(): jnp.where(is_encoder, late_all, early_all)]
    concatenate x2 -> x0, other arithmetic: 4.5 us -> none  [the longest x1 3.82 us: own_entries(): window = jnp.concatenate(lower, axis=-1)]
  transfers between devices with their start and end apart: 3 -> 4, of which waited for: 2 -> 4; matrix products, arithmetic and copies ran while one was open for 8% -> 4% of each run, Pallas kernels for 0% -> 0%
where the time goes in v2:
time: 158 us
  waiting for transfers between devices  76.6 us (48%)
  starting transfers between devices  23.1 us (15%)
  between operations  18.6 us (12%)
  blocking collectives  17.9 us (11%)
  local copies, waits for them, and re-layouts  7.75 us (5%)
  other arithmetic  6.89 us (4%)
  matrix products  6.44 us (4%)
    all_gather x1, waiting for transfers between devices, local(): late_all = lax.all_gather(late, axes, axis=0)  59.1 us
    ppermute x2, starting transfers between devices, shifted(): return lax.ppermute(block, axis, route)  23 us
    all_gather x2, blocking collectives, halo_block(): gathered = lax.all_gather(both_rows[None], 'tile', axis=0, tiled=True)  17.9 us
    all_gather x1, waiting for transfers between devices, local(): early_all = lax.all_gather(early, axes, axis=0)  15.3 us
    dot_general x2, matrix products, front(): return jnp.dot(patch_mat, forward_mat, preferred_element_type=jnp.float32)  3.73 us
  transfers between devices with their start and end apart: 4, of which 4 were waited for; matrix products, arithmetic and copies ran while one was open for 4% of the time, Pallas kernels for 0%

profile of v2, /device:TPU:0, one launch (start us, length us, event | category | flops | bytes accessed | tf_op | source)
XLA Modules:
  0.0 157.5 jit_solution(12969855877124781496)
XLA Ops:
  7.2 1.3 fusion.99
  12.5 0.9 squeeze.31
  13.4 0.1 broadcast_and_fusion
  13.4 0.1 copy.140
  13.6 1.1 fusion.78
  14.7 9.7 %all-gather = bf16[12,2,4,256]{3,2,1,0:T(4,128)(2,1)S(1)} all-gather(bf16[3,2,4,256]{3,2,1,0:T(4,128)(2,1)S(1)} %copy.131), channel_id=2, replica_groups=mesh['segment'=2,'clip'=4,'tile'=4] {'tile'}, dimensions={0}, use_global_device_ids=true | all-gather | bytes 61440 | tf_op jit(solution)/shard_map/all_gather | solution.py:128
  24.5 0.1 pad.42.clone
  24.6 0.1 maximum_maximum_fusion
  24.7 0.1 dynamic_update_slice.6
  24.8 0.1 broadcast_in_dim.84
  24.9 0.1 broadcast_select_fusion.2
  25.0 0.7 pad_select_fusion.1
  25.8 3.0 %conditional.1 = (f32[3,12,4,256]{3,1,2,0:T(8,128)S(1)}) conditional(s32[]{:T(128)} %convert_element_type.40, (bf16[3,14,6,256]{3,1,2,0:T(8,128)(2,1)S(1)}, bf16[1,27,256,256]{3,2,1,0:T(8,128)(2,1)}) %tuple.16, (bf16[3,14,6,256]{3,1,2,0:T(8,128)(2,1)S(1)}, bf16[6912,256]{1,0:T(8,128)(2,1)}) %tuple.48), branch_computations={%region_0.1_spmd, %region_1.2_spmd} | conditional | flops 509607936 | bytes 26007588 | solution.py:156
  26.5 1.4 copy-done
  27.9 0.9 fusion.18
  28.8 0.1 fusion.61
  28.9 21.5 %collective-permute-start = (bf16[3,12,4,256]{3,1,2,0:T(8,128)(2,1)S(1)}, bf16[3,12,4,256]{3,1,2,0:T(8,128)(2,1)S(1)}, u32[]{:S(2)}, u32[]{:S(2)}) collective-permute-start(bf16[3,12,4,256]{3,1,2,0:T(8,128)(2,1)S(1)} %fusion.61), channel_id=1, source_target_pairs={{0,16},{1,17},{2,18},{3,19},{4,20},{5,21},{6,22},{7,23},{8,24},{9,... | collective-permute-start | bytes 221192 | tf_op jit(solution)/shard_map/ppermute | solution.py:12
  50.5 0.1 dynamic-slice.1
  50.6 0.1 dynamic-slice
  50.7 0.7 collective-permute-done
  51.3 0.1 fusion.71
  51.6 8.2 %all-gather.1 = bf16[12,2,4,256]{3,2,1,0:T(4,128)(2,1)S(1)} all-gather(bf16[3,2,4,256]{3,2,1,0:T(4,128)(2,1)S(1)} %copy.136), channel_id=3, replica_groups=mesh['segment'=2,'clip'=4,'tile'=4] {'tile'}, dimensions={0}, use_global_device_ids=true | all-gather | bytes 61440 | tf_op jit(solution)/shard_map/all_gather | solution.py:128
  59.8 0.1 maximum_maximum_fusion.1
  59.9 0.1 dynamic_update_slice.7
  60.1 1.5 collective-permute-start.1
  61.7 1.5 collective-permute-done.1
  63.3 0.7 pad_select_fusion
  64.5 2.9 %fusion.53 = bf16[1,1,1,3,12,4,256]{6,4,5,3,2,1,0:T(8,128)(2,1)S(1)} fusion(bf16[3,12,4,256]{3,1,2,0:T(8,128)(2,1)S(1)} %fusion.61, bf16[3,12,4,6912]{3,1,2,0:T(8,128)(2,1)S(1)} %slice_dynamic-update-slice_fusion.21, bf16[6912,256,1,1]{1,0,3,2:T(8,128)(2,1)} %bitcast.103, bf16[3,12,4,256]{3,1,2,0:T(8,128)(2,1)S(1)} %collective-permute-done, ...), kind=kOutput, calls=%fused_computation.112 | convolution fusion | flops 509792256 | bytes 5750833 | tf_op jit(solution)/shard_map/dot_general | solution.py:138
  67.3 0.7 copy.150
  68.0 15.3 %all-gather.7.cloned.1.call-done = bf16[2688,256]{1,0:T(8,128)(2,1)} async-done(((bf16[168,256]{1,0:T(8,128)(2,1)}), bf16[2688,256]{1,0:T(8,128)(2,1)}) %all-gather.7.cloned.1.call-update) | async-done | bytes 1376272 | tf_op jit(solution)/shard_map/all_gather | solution.py:155
  83.3 59.1 %all-gather.9.cloned.1.call-done = bf16[2688,256]{1,0:T(8,128)(2,1)} async-done(((bf16[168,256]{1,0:T(8,128)(2,1)}), bf16[2688,256]{1,0:T(8,128)(2,1)}) %all-gather.9.cloned.1.call-update) | async-done | bytes 1376272 | tf_op jit(solution)/shard_map/all_gather | solution.py:166
  142.4 1.9 %broadcast_select_fusion = (bf16[2688,256]{1,0:T(8,128)(2,1)S(1)}, bf16[2688,256]{1,0:T(8,128)(2,1)S(1)}) fusion(bf16[2688,256]{1,0:T(8,128)(2,1)} %all-gather.9.cloned.1.call-done, bf16[2688,256]{1,0:T(8,128)(2,1)} %all-gather.7.cloned.1.call-done, pred[]{:T(512)S(6)} %eq.8), kind=kLoop, calls=%fused_computation.100 | loop fusion | flops 1376256 | bytes 5505025 | tf_op jit(solution)/shard_map/jit(_where)/select_n | solution.py:172
  144.4 0.1 slice.336
  144.5 1.3 fusion.39
  145.8 0.6 fusion.44
  146.4 0.4 convolution_bitcast_fusion.3
  146.8 0.6 fusion.47
  147.4 0.4 convolution_bitcast_fusion.2
  147.8 0.3 convolution_bitcast_fusion.1
  148.2 0.3 convolution_bitcast_fusion
  148.5 0.1 fusion.73
  148.6 0.2 copy.162
  148.8 0.1 fusion.75
  148.8 0.2 copy.161
  149.0 0.1 fusion.77
  149.0 0.2 copy.160
  149.2 0.4 pad_maximum_fusion
  149.6 1.1 broadcast_in_dim.89
  (87 shorter events, 1.5 us)
Async XLA Ops:
  7.2 76.1 %all-gather.7.cloned.1.call-start = ((), (), s32[]{:S(2)}) async-start(), calls=%async_computation | async-start | bytes 1462272 | tf_op jit(solution)/shard_map/all_gather | solution.py:155
  25.7 116.7 %all-gather.9.cloned.1.call-start = ((), (), s32[]{:S(2)}) async-start(), calls=%async_computation.1 | async-start | bytes 1462272 | tf_op jit(solution)/shard_map/all_gather | solution.py:166
  25.8 3.0 %copy-start.2 = (bf16[1,1,3,12,4,256]{5,4,3,2,1,0:T(4,128)(2,1)S(1)}, bf16[1,1,3,12,4,256]{5,4,3,2,1,0:T(4,128)(2,1)}, u32[]{:S(2)}) copy-start(bf16[1,1,3,12,4,256]{5,4,3,2,1,0:T(4,128)(2,1)} %param.8) | copy-start | bytes 221188
  25.8 25.5 %copy-start.1 = (bf16[1,1,3,12,4,256]{5,4,3,2,1,0:T(4,128)(2,1)S(1)}, bf16[1,1,3,12,4,256]{5,4,3,2,1,0:T(4,128)(2,1)}, u32[]{:S(2)}) copy-start(bf16[1,1,3,12,4,256]{5,4,3,2,1,0:T(4,128)(2,1)} %param.9) | copy-start | bytes 221188
  25.9 2.0 %copy-start = (bf16[6912,256]{1,0:T(8,128)(2,1)S(1)}, bf16[6912,256]{1,0:T(8,128)(2,1)}, u32[]{:S(2)}) copy-start(bf16[6912,256]{1,0:T(8,128)(2,1)} %get-tuple-element.16) | copy-start | bytes 10616836 | tf_op jit(solution)/shard_map/cond
  28.9 22.5 %collective-permute-start = (bf16[3,12,4,256]{3,1,2,0:T(8,128)(2,1)S(1)}, bf16[3,12,4,256]{3,1,2,0:T(8,128)(2,1)S(1)}, u32[]{:S(2)}, u32[]{:S(2)}) collective-permute-start(bf16[3,12,4,256]{3,1,2,0:T(8,128)(2,1)S(1)} %fusion.61), channel_id=1, source_target_pairs={{0,16},{1,17},{2,18},{3,19},{4,20},{5,21},{6,22},{7,23},{8,24},{9,... | collective-permute-start | bytes 221192 | tf_op jit(solution)/shard_map/ppermute | solution.py:12
  60.1 3.2 %collective-permute-start.1 = (bf16[3,12,4,256]{3,1,2,0:T(8,128)(2,1)S(1)}, bf16[3,12,4,256]{3,1,2,0:T(8,128)(2,1)S(1)}, u32[]{:S(2)}, u32[]{:S(2)}) collective-permute-start(bf16[3,12,4,256]{3,1,2,0:T(8,128)(2,1)S(1)} %get-tuple-element.48), channel_id=1, source_target_pairs={{16,0},{17,1},{18,2},{19,3},{20,4},{21,5},{22,6},{23,7},{24,8},{25... | collective-permute-start | bytes 221192 | tf_op jit(solution)/shard_map/ppermute | solution.py:12
Sparse Core Ops, SparseCore 0:
  25.8 57.4 all-gather.6
  86.7 55.7 all-gather.8

commit v3 on v2

--- a/solution.py
+++ b/solution.py
@@ -1,3 +1,5 @@
+import functools
+
 import jax
 import jax.numpy as jnp
 from jax import lax
@@ -5,6 +7,8 @@
 from jax.experimental.pallas import tpu as pltpu
 from jax.sharding import PartitionSpec as P
 
+MESH = pl.DeviceIdType.MESH
+
 
 def shifted(block, axis, distance):
     devices = range(lax.axis_size(axis))
@@ -25,43 +29,123 @@
     return jnp.pad(padded, ((0, 0), (0, 0), (1, 1), (0, 0)))
 
 
-def patches(stacked, frame_count, height, columns):
-    pieces = []
-    for depth_off in range(3):
-        for row_off in range(3):
-            for col_off in range(3):
-                pieces.append(
-                    stacked[
-                        depth_off : depth_off + frame_count,
-                        row_off : row_off + height,
-                        col_off : col_off + columns,
-                    ]
-                )
-    return jnp.concatenate(pieces, axis=-1).reshape(frame_count * height * columns, -1)
-
-
-def back_kernel(patch_ref, weight_ref, out_ref):
+def conv_kernel(both, patch_ref, weight_ref, out_ref):
     taps, channels = weight_ref.shape[0], weight_ref.shape[2]
-    total = jnp.zeros(out_ref.shape, jnp.float32)
-    for tap in range(taps):
-        total += lax.dot_general(
-            patch_ref[:, tap * channels : (tap + 1) * channels],
-            weight_ref[taps - 1 - tap],
-            (((1,), (1,)), ((), ())),
-            preferred_element_type=jnp.float32,
-        )
-    out_ref[...] = total
-
-
-def conv_back_dot(patch_mat, kernel):
-    rows, channels = patch_mat.shape[0], kernel.shape[1]
+    rows = out_ref.shape[0]
+    frame_rows = (patch_ref.shape[0] - rows) // 2
+
+    def run(backward):
+        total = jnp.zeros(out_ref.shape, jnp.float32)
+        for tap in range(taps):
+            low, place = tap // 9 * frame_rows, tap % 9 * channels
+            total += lax.dot_general(
+                patch_ref[low : low + rows, place : place + channels],
+                weight_ref[taps - 1 - tap if backward else tap],
+                (((1,), (1 if backward else 0,)), ((), ())),
+                preferred_element_type=jnp.float32,
+            )
+        out_ref[...] = total
+
+    if both:
+        section = lax.axis_index("segment")
+        pl.when(section == 0)(lambda: run(False))
+        pl.when(section != 0)(lambda: run(True))
+    else:
+        run(False)
+
+
+def conv_dot(patch_mat, kernel, both):
+    channels = kernel.shape[1]
+    rows = patch_mat.shape[0] * 3 // 5
     return pl.pallas_call(
-        back_kernel,
+        functools.partial(conv_kernel, both),
         out_shape=jax.ShapeDtypeStruct((rows, channels), jnp.float32),
         in_specs=[pl.BlockSpec(memory_space=pltpu.VMEM)] * 2,
         out_specs=pl.BlockSpec(memory_space=pltpu.VMEM),
         compiler_params=pltpu.CompilerParams(vmem_limit_bytes=24 * 2**20),
     )(patch_mat, kernel)
+
+
+def spatial_patches(stacked, height, columns):
+    pieces = [
+        stacked[:, row_off : row_off + height, col_off : col_off + columns]
+        for row_off in range(3)
+        for col_off in range(3)
+    ]
+    return jnp.concatenate(pieces, axis=-1).reshape(stacked.shape[0] * height * columns, -1)
+
+
+def gather_kernel(clips, tiles, own_ref, all_ref, send_sem, recv_sem, local_sem):
+    section = lax.axis_index("segment")
+    clip = lax.axis_index("clip")
+    tile = lax.axis_index("tile")
+    clip_peers = [lax.rem(clip + step, clips) for step in range(1, clips)]
+    tile_peers = [lax.rem(tile + step, tiles) for step in range(1, tiles)]
+    places = [(section, peer, tile) for peer in clip_peers]
+    places += [(section, clip, peer) for peer in tile_peers]
+
+    barrier = pltpu.get_barrier_semaphore()
+    for place in places:
+        pl.semaphore_signal(barrier, inc=1, device_id=place, device_id_type=MESH)
+    pl.semaphore_wait(barrier, len(places))
+
+    def send(source, slot_clip, number, place):
+        copy = pltpu.make_async_remote_copy(
+            src_ref=source,
+            dst_ref=all_ref.at[slot_clip, tile],
+            send_sem=send_sem.at[number],
+            recv_sem=recv_sem.at[slot_clip, tile],
+            device_id=place,
+            device_id_type=MESH,
+        )
+        copy.start()
+        return copy
+
+    def arrived(slot_clip, slot_tile):
+        slot = all_ref.at[slot_clip, slot_tile]
+        pltpu.make_async_remote_copy(
+            src_ref=slot,
+            dst_ref=slot,
+            send_sem=send_sem.at[0],
+            recv_sem=recv_sem.at[slot_clip, slot_tile],
+            device_id=places[0],
+            device_id_type=MESH,
+        ).wait_recv()
+
+    own = pltpu.make_async_copy(own_ref, all_ref.at[clip, tile], local_sem)
+    own.start()
+    copies = [send(own_ref, clip, number, place) for number, place in enumerate(places)]
+    for peer in clip_peers:
+        arrived(peer, tile)
+        for other in tile_peers:
+            copies.append(send(all_ref.at[peer, tile], peer, len(copies), (section, clip, other)))
+    for other in tile_peers:
+        arrived(clip, other)
+    for peer in clip_peers:
+        for other in tile_peers:
+            arrived(peer, other)
+    own.wait()
+    for copy in copies:
+        copy.wait_send()
+
+
+def gather_all(block):
+    clips, tiles = lax.axis_size("clip"), lax.axis_size("tile")
+    gathered = pl.pallas_call(
+        functools.partial(gather_kernel, clips, tiles),
+        out_shape=jax.ShapeDtypeStruct((clips, tiles) + block.shape, block.dtype),
+        in_specs=[pl.BlockSpec(memory_space=pltpu.VMEM)],
+        out_specs=pl.BlockSpec(memory_space=pltpu.VMEM),
+        scratch_shapes=[
+            pltpu.SemaphoreType.DMA((clips * tiles - 1,)),
+            pltpu.SemaphoreType.DMA((clips, tiles)),
+            pltpu.SemaphoreType.DMA,
+        ],
+        compiler_params=pltpu.CompilerParams(
+            collective_id=0, has_side_effects=True, vmem_limit_bytes=32 * 2**20
+        ),
+    )(block)
+    return gathered.reshape((clips * tiles,) + block.shape)
 
 
 def own_entries(acts, ups, axes, frame_count, height, columns):
@@ -118,7 +202,6 @@
     inside = (row_ids[:, None] < row_count) & (col_ids[None, :] < col_count)
     inside_mask = inside[None, :, :, None]
     kernel = weights[0]
-    forward_mat = kernel.reshape(27 * channels, channels)
     front_zero = jnp.zeros((2, height + 2, columns + 2, channels), jnp.bfloat16)
 
     def halo_block(field):
@@ -132,15 +215,6 @@
         bottom = jnp.where(lower_tile < tile_count, bottom, jnp.zeros_like(bottom))
         return pad_block(field, upper, bottom, row_count)
 
-    def front(padded):
-        stacked = jnp.concatenate([front_zero, padded], axis=0)
-        patch_mat = patches(stacked, frame_count, height, columns)
-        return jnp.dot(patch_mat, forward_mat, preferred_element_type=jnp.float32)
-
-    def back(padded):
-        stacked = jnp.concatenate([padded, front_zero], axis=0)
-        return conv_back_dot(patches(stacked, frame_count, height, columns), kernel)
-
     def flat(field):
         rows = field.reshape(-1, channels)
         return jnp.pad(rows, ((0, frame_count * (height + 2) * columns - rows.shape[0]), (0, 0)))
@@ -153,7 +227,12 @@
     padded = halo_block(jnp.where(is_encoder, active, target))
     early = jnp.where(is_encoder, flat(padded[:, :, 1:-1]), flat(target))
     early_all = lax.all_gather(early, axes, axis=0)
-    mixed = lax.cond(is_encoder, front, back, padded).reshape(target.shape)
+    stacked = jnp.where(
+        is_encoder,
+        jnp.concatenate([front_zero, padded], axis=0),
+        jnp.concatenate([padded, front_zero], axis=0),
+    )
+    mixed = conv_dot(spatial_patches(stacked, height, columns), kernel, True).reshape(target.shape)
     hidden = jnp.where(inside_mask, source.astype(jnp.float32) + mixed, 0.0).astype(jnp.bfloat16)
     latent = shifted(hidden, "segment", 1)
     wide = latent.astype(jnp.float32)
@@ -163,9 +242,11 @@
     returned = shifted(own_grad, "segment", -1)
     padded_two = halo_block(jax.nn.silu(wide).astype(jnp.bfloat16))
     late = jnp.where(is_encoder, flat(returned), flat(padded_two[:, :, 1:-1]))
-    late_all = lax.all_gather(late, axes, axis=0)
+    late_all = gather_all(late)
+    stacked = jnp.concatenate([front_zero, padded_two], axis=0)
+    second = conv_dot(spatial_patches(stacked, height, columns), kernel, False)
     decoded = jnp.where(
-        inside_mask, wide + front(padded_two).reshape(target.shape), 0.0
+        inside_mask, wide + second.reshape(target.shape), 0.0
     ).astype(jnp.bfloat16)
     own_out = jnp.where(is_encoder, hidden, decoded)
     acts = jnp.where(is_encoder, early_all, late_all)

time: 158 us -> 114 us (0.72)
  waiting for transfers between devices: 76.6 us -> 0.04 us
  Pallas kernels: 0 us -> 27.9 us
  local copies, waits for them, and re-layouts: 7.75 us -> 30.7 us
  starting transfers between devices: 23.1 us -> 3.24 us
  other arithmetic: 6.89 us -> 11.7 us
  matrix products: 6.44 us -> 2.7 us
    all_gather x1 -> x0, waiting for transfers between devices: 59.1 us -> none  [local(): late_all = lax.all_gather(late, axes, axis=0)]
    pallas_call x0 -> x3, Pallas kernels: none -> 27.9 us  [the longest x1 26.5 us: gather_all(): pl.pallas_call(functools.partial(gather_kernel, clips, tiles), out_shape=...]
    ppermute x2, starting transfers between devices: 23 us -> 3.2 us  [shifted(): return lax.ppermute(block, axis, route)]
    all_gather x1, waiting for transfers between devices: 15.3 us -> 0.02 us  [local(): early_all = lax.all_gather(early, axes, axis=0)]
    unnamed x34 -> x33, local copies, waits for them, and re-layouts: 1.57 us -> 16.1 us
    reshape x0 -> x4, local copies, waits for them, and re-layouts: none -> 6.93 us  [the longest x2 4.37 us: spatial_patches(): jnp.concatenate(pieces, axis=-1)]
    dot_general x2 -> x0, matrix products: 3.73 us -> none  [front(): return jnp.dot(patch_mat, forward_mat, preferred_element_type=jnp.float32)]
    ppermute x2, waiting for transfers between devices: 2.15 us -> 0.01 us  [shifted(): return lax.ppermute(block, axis, route)]
  transfers between devices with their start and end apart: 4 -> 3, of which waited for: 4 -> 0; matrix products, arithmetic and copies ran while one was open for 4% -> 25% of each run, Pallas kernels for 0% -> 25%
where the time goes in v3:
time: 114 us; the launch traced here: 113 us
  local copies, waits for them, and re-layouts  30.7 us (27%)
  Pallas kernels  27.9 us (24%)
  between operations  18.3 us (16%)
  blocking collectives  18.2 us (16%)
  other arithmetic  11.7 us (10%)
  starting transfers between devices  3.24 us (3%)
  matrix products  2.7 us (2%)
    pallas_call x1, Pallas kernels, gather_all(): pl.pallas_call(functools.partial(gather_kernel, clips, tiles), out_shape=...  26.5 us
    all_gather x2, blocking collectives, halo_block(): gathered = lax.all_gather(both_rows[None], 'tile', axis=0, tiled=True)  18.2 us
    unnamed x33, local copies, waits for them, and re-layouts  16.1 us
    reshape x2, local copies, waits for them, and re-layouts, spatial_patches(): jnp.concatenate(pieces, axis=-1)  4.37 us
    ppermute x2, starting transfers between devices, shifted(): return lax.ppermute(block, axis, route)  3.2 us
    dot_general x6, matrix products, own_entries(): lax.dot_general(acts[:, :count], moved[:, frame_count - count:], contract...  2.7 us
  transfers between devices with their start and end apart: 3, of which 0 were waited for; matrix products, arithmetic and copies ran while one was open for 25% of the time, Pallas kernels for 25%

profile of v3, /device:TPU:0, one launch (start us, length us, event | category | flops | bytes accessed | tf_op | source)
XLA Modules:
  0.0 112.8 jit_solution(10939322301797512781)
XLA Ops:
  7.2 1.3 %fusion.51 = (s32[1,1,1]{2,1,0:T(1,128)}, s32[1,1,1]{2,1,0:T(1,128)}) fusion(s32[1,1,2]{2,1,0:T(1,128)} %param.9), kind=kLoop, calls=%fused_computation.112 | loop fusion | bytes 16 | tf_op jit(solution)/shard_map/slice | solution.py:199
  12.7 0.9 squeeze.31
  13.6 1.1 fusion.46
  14.7 9.7 %all-gather = bf16[12,2,4,256]{3,2,1,0:T(4,128)(2,1)S(1)} all-gather(bf16[3,2,4,256]{3,2,1,0:T(4,128)(2,1)S(1)} %pad_maximum_fusion.1), channel_id=2, replica_groups=mesh['segment'=2,'clip'=4,'tile'=4] {'tile'}, dimensions={0}, use_global_device_ids=true | all-gather | bytes 61440 | tf_op jit(solution)/shard_map/all_gather | solution.py:211
  24.8 0.7 pad_select_fusion.2
  25.6 0.7 slice_dynamic-update-slice_fusion.8
  26.3 0.7 slice_dynamic-update-slice_fusion.7
  27.0 0.8 slice_dynamic-update-slice_fusion.6
  27.8 0.7 slice_dynamic-update-slice_fusion.5
  28.5 0.8 slice_dynamic-update-slice_fusion.4
  29.3 0.7 slice_dynamic-update-slice_fusion.3
  30.0 0.7 slice_dynamic-update-slice_fusion.2
  30.7 0.7 slice_dynamic-update-slice_fusion.1
  31.4 0.7 slice_dynamic-update-slice_fusion
  32.2 2.2 %reshape.184.patch_ref = bf16[240,2304]{1,0:T(8,128)(2,1)} reshape(bf16[5,12,4,2304]{3,2,1,0:T(4,128)(2,1)} %slice_dynamic-update-slice_fusion) | data formatting | bytes 2211840 | tf_op jit(solution)/shard_map/reshape | solution.py:75
  34.4 1.3 %copy-done.1 = bf16[240,2304]{1,0:T(8,128)(2,1)S(1)} copy-done((bf16[240,2304]{1,0:T(8,128)(2,1)S(1)}, bf16[240,2304]{1,0:T(8,128)(2,1)}, u32[]{:S(2)}) %copy-start.1) | copy-done | bytes 1105944
  35.6 0.7 shard_map.77
  36.3 0.7 copy-done.3
  37.0 1.6 %reshape.185 = f32[3,12,4,256]{3,2,1,0:T(4,128)} reshape(f32[144,256]{1,0:T(8,128)} %copy-done.3) | data formatting | bytes 294912 | tf_op jit(solution)/shard_map/reshape | solution.py:235
  38.6 1.7 %fusion.18 = bf16[3,12,4,256]{3,2,1,0:T(4,128)(2,1)} fusion(f32[3,12,4,256]{3,2,1,0:T(4,128)} %reshape.185, pred[12,4]{1,0:T(8,128)(4,1)S(1)} %broadcast_and_fusion, bf16[1,1,3,12,4,256]{5,4,3,2,1,0:T(4,128)(2,1)} %param.6), kind=kLoop, calls=%fused_computation.49 | loop fusion | flops 184320 | bytes 294960 | tf_op jit(solution)/shard_map/convert_element_type | solution.py:236
  40.3 1.9 %collective-permute-start = (bf16[3,12,4,256]{3,2,1,0:T(4,128)(2,1)}, bf16[3,12,4,256]{3,2,1,0:T(4,128)(2,1)}, u32[]{:S(2)}, u32[]{:S(2)}) collective-permute-start(bf16[3,12,4,256]{3,2,1,0:T(4,128)(2,1)} %fusion.18), channel_id=1, source_target_pairs={{0,16},{1,17},{2,18},{3,19},{4,20},{5,21},{6,22},{7,23},{8,24},{9,... | collective-permute-start | bytes 221192 | tf_op jit(solution)/shard_map/ppermute | solution.py:16
  42.8 0.7 dynamic-slice
  43.5 1.8 %fusion.30 = (bf16[3,12,4,256]{3,2,1,0:T(4,128)(2,1)}, bf16[3,12,4,256]{3,2,1,0:T(4,128)(2,1)S(1)}) fusion(f32[3,12,4,256]{3,2,1,0:T(4,128)} %reshape.185, bf16[3,12,4,256]{3,2,1,0:T(4,128)(2,1)} %collective-permute-done, pred[12,4]{1,0:T(8,128)(4,1)S(1)} %broadcast_and_fusion, bf16[1,1,3,12,4,256]{5,4,3,2,1,0:T(4,128)(2,1)} %param.7), kind=kLoop, calls=%fused_computation.61 | loop fusion | flops 589824 | bytes 442416 | tf_op jit(solution)/shard_map/convert_element_type | solution.py:241
  45.3 1.3 %collective-permute-start.1 = (bf16[3,12,4,256]{3,2,1,0:T(4,128)(2,1)}, bf16[3,12,4,256]{3,2,1,0:T(4,128)(2,1)}, u32[]{:S(2)}, u32[]{:S(2)}) collective-permute-start(bf16[3,12,4,256]{3,2,1,0:T(4,128)(2,1)} %get-tuple-element.4), channel_id=1, source_target_pairs={{16,0},{17,1},{18,2},{19,3},{20,4},{21,5},{22,6},{23,7},{24,8},{25... | collective-permute-start | bytes 221192 | tf_op jit(solution)/shard_map/ppermute | solution.py:16
  46.7 8.5 %all-gather.1 = bf16[12,2,4,256]{3,2,1,0:T(4,128)(2,1)S(1)} all-gather(bf16[3,2,4,256]{3,2,1,0:T(4,128)(2,1)S(1)} %pad_maximum_fusion.2), channel_id=3, replica_groups=mesh['segment'=2,'clip'=4,'tile'=4] {'tile'}, dimensions={0}, use_global_device_ids=true | all-gather | bytes 61440 | tf_op jit(solution)/shard_map/all_gather | solution.py:211
  55.3 0.7 fusion.38
  56.1 0.7 fusion.39
  56.8 0.7 fusion.40
  57.5 0.7 fusion.41
  58.2 0.7 fusion.42
  59.0 0.7 fusion.43
  59.7 0.7 fusion.44
  60.4 0.7 fusion.45
  61.1 0.7 fusion.37
  61.9 2.2 %reshape.186.patch_ref = bf16[240,2304]{1,0:T(8,128)(2,1)} reshape(bf16[5,12,4,2304]{3,2,1,0:T(4,128)(2,1)} %fusion.37) | data formatting | bytes 2211840 | tf_op jit(solution)/shard_map/reshape | solution.py:75
  64.1 1.2 %copy-done.2 = bf16[240,2304]{1,0:T(8,128)(2,1)S(1)} copy-done((bf16[240,2304]{1,0:T(8,128)(2,1)S(1)}, bf16[240,2304]{1,0:T(8,128)(2,1)}, u32[]{:S(2)}) %copy-start.2) | copy-done | bytes 1105944
  65.3 0.7 shard_map.78
  66.0 0.7 copy-done.4
  66.7 1.0 reshape.187
  67.6 1.7 %fusion.48 = bf16[1,1,1,3,12,4,256]{6,5,4,3,2,1,0:T(4,128)(2,1)} fusion(bf16[3,12,4,256]{3,2,1,0:T(4,128)(2,1)} %fusion.18, f32[3,12,4,256]{3,2,1,0:T(4,128)S(1)} %reshape.187, bf16[3,12,4,256]{3,2,1,0:T(4,128)(2,1)} %collective-permute-done, pred[12,4]{1,0:T(8,128)(4,1)S(1)} %broadcast_and_fusion, pred[]{:T(512)S(6)} %eq.8), kind=kLoop, calls=%fused_computation.92 | loop fusion | flops 184320 | bytes 368689 | tf_op jit(solution)/shard_map/broadcast_in_dim | solution.py:255
  69.3 0.9 reshape.190
  70.3 0.9 reshape.189
  71.2 26.5 %shard_map.79 = bf16[4,4,168,256]{3,2,1,0:T(8,128)(2,1)S(1)} custom-call(bf16[168,256]{1,0:T(8,128)(2,1)S(1)} %pad_select_fusion.1.own_ref), custom_call_target="tpu_custom_call" | custom-call | tf_op jit(solution)/shard_map/pallas_call | solution.py:134
  97.8 1.6 %broadcast_select_fusion = bf16[16,168,256]{2,1,0:T(8,128)(2,1)S(1)} fusion(bf16[16,168,256]{2,1,0:T(8,128)(2,1)} %bitcast.108, pred[]{:T(512)S(6)} %eq.8, bf16[4,4,168,256]{3,2,1,0:T(8,128)(2,1)S(1)} %shard_map.79), kind=kLoop, calls=%fused_computation.8 | loop fusion | flops 688128 | bytes 4128769 | tf_op jit(solution)/shard_map/jit(_where)/select_n | solution.py:252
  99.7 1.3 %fusion.1 = (bf16[16,3,56,256]{3,2,0,1:T(8,128)(2,1)S(1)}, bf16[16,3,56,256]{3,2,0,1:T(8,128)(2,1)S(1)}) fusion(s32[]{:T(128)S(6)} %select_n.238, pred[56]{0:T(512)(128)(4,1)S(1)} %dynamic-slice.1, s32[]{:T(128)S(6)} %select_n.234, pred[56]{0:T(512)(128)(4,1)S(1)} %dynamic-slice, bf16[16,3,48,256]{3,2,1,0:T(8,128)(2,1)S(1)} %bitcast.110), kind=kLoop, calls=%fused_computation.3 | loop fusion | flops 1376256 | bytes 3932280 | tf_op jit(solution)/shard_map/jit(_where)/select_n | solution.py:167
  101.8 0.6 fusion.9
  103.2 0.6 fusion.6
  104.8 1.1 broadcast_in_dim.87
  (50 shorter events, 4.4 us)
Async XLA Ops:
  7.2 90.6 %all-gather.5.cloned.1.call-start = ((), (), s32[]{:S(2)}) async-start(), calls=%async_computation | async-start | bytes 1462272 | tf_op jit(solution)/shard_map/all_gather | solution.py:229
  27.8 6.6 %copy-start = (bf16[1,27,256,256]{3,2,1,0:T(8,128)(2,1)S(1)}, bf16[1,27,256,256]{3,2,1,0:T(8,128)(2,1)}, u32[]{:S(2)}) copy-start(bf16[1,27,256,256]{3,2,1,0:T(8,128)(2,1)} %param.8) | copy-start | bytes 10616836
  34.4 1.3 %copy-start.1 = (bf16[240,2304]{1,0:T(8,128)(2,1)S(1)}, bf16[240,2304]{1,0:T(8,128)(2,1)}, u32[]{:S(2)}) copy-start(bf16[240,2304]{1,0:T(8,128)(2,1)} %reshape.184.patch_ref) | copy-start | bytes 3317764
  36.3 0.7 copy-start.3
  40.3 3.2 %collective-permute-start = (bf16[3,12,4,256]{3,2,1,0:T(4,128)(2,1)}, bf16[3,12,4,256]{3,2,1,0:T(4,128)(2,1)}, u32[]{:S(2)}, u32[]{:S(2)}) collective-permute-start(bf16[3,12,4,256]{3,2,1,0:T(4,128)(2,1)} %fusion.18), channel_id=1, source_target_pairs={{0,16},{1,17},{2,18},{3,19},{4,20},{5,21},{6,22},{7,23},{8,24},{9,... | collective-permute-start | bytes 221192 | tf_op jit(solution)/shard_map/ppermute | solution.py:16
  45.3 24.9 %collective-permute-start.1 = (bf16[3,12,4,256]{3,2,1,0:T(4,128)(2,1)}, bf16[3,12,4,256]{3,2,1,0:T(4,128)(2,1)}, u32[]{:S(2)}, u32[]{:S(2)}) collective-permute-start(bf16[3,12,4,256]{3,2,1,0:T(4,128)(2,1)} %get-tuple-element.4), channel_id=1, source_target_pairs={{16,0},{17,1},{18,2},{19,3},{20,4},{21,5},{22,6},{23,7},{24,8},{25... | collective-permute-start | bytes 221192 | tf_op jit(solution)/shard_map/ppermute | solution.py:16
  55.3 5.8 %copy-start.5 = (bf16[3,14,4,256]{3,2,1,0:T(4,128)(2,1)}, bf16[3,14,4,256]{3,2,1,0:T(4,128)(2,1)S(1)}, u32[]{:S(2)}) copy-start(bf16[3,14,4,256]{3,2,1,0:T(4,128)(2,1)S(1)} %bitcast_dynamic-update-slice_fusion) | copy-start | bytes 258052
  64.1 1.2 %copy-start.2 = (bf16[240,2304]{1,0:T(8,128)(2,1)S(1)}, bf16[240,2304]{1,0:T(8,128)(2,1)}, u32[]{:S(2)}) copy-start(bf16[240,2304]{1,0:T(8,128)(2,1)} %reshape.186.patch_ref) | copy-start | bytes 3317764
  66.0 0.7 copy-start.4
  97.8 1.8 %copy-start.6 = (bf16[2688,256]{1,0:T(8,128)(2,1)S(1)}, bf16[2688,256]{1,0:T(8,128)(2,1)}, u32[]{:S(2)}) copy-start(bf16[2688,256]{1,0:T(8,128)(2,1)} %all-gather.5.cloned.1.call-done) | copy-start | bytes 4128772
Sparse Core Ops, SparseCore 0:
  25.6 61.4 all-gather.4

commit v4 on v3

--- a/solution.py
+++ b/solution.py
@@ -21,29 +21,54 @@
     return sigmoid * (1.0 + values * (1.0 - sigmoid))
 
 
-def pad_block(strip_field, upper, bottom, row_count):
-    frame_count, height, columns, channels = strip_field.shape
-    blank = jnp.zeros((frame_count, 1, columns, channels), strip_field.dtype)
-    padded = jnp.concatenate([upper[:, None], strip_field, blank], axis=1)
-    padded = lax.dynamic_update_slice_in_dim(padded, bottom[:, None], row_count + 1, axis=1)
-    return jnp.pad(padded, ((0, 0), (0, 0), (1, 1), (0, 0)))
-
-
-def conv_kernel(both, patch_ref, weight_ref, out_ref):
+def conv_kernel(both, columns, field_ref, weight_ref, out_ref, wide, taps_mat):
     taps, channels = weight_ref.shape[0], weight_ref.shape[2]
     rows = out_ref.shape[0]
-    frame_rows = (patch_ref.shape[0] - rows) // 2
+    frame_rows = taps_mat.shape[1] // 5
+    tall = frame_rows + 2 * columns
+    field_rows = field_ref.shape[0]
+    lead = 8
 
     def run(backward):
+        wide[...] = jnp.zeros(wide.shape, jnp.float32)
+        first = lead if backward else lead + 2 * tall
+        wide[first : first + field_rows] = field_ref[...].astype(jnp.float32)
+        column = lax.broadcasted_iota(jnp.int32, (frame_rows, channels), 0) % columns
+        for frame in range(5):
+            for row_off in range(3):
+                for col_off in range(3):
+                    start = lead + tall * frame + columns * row_off + col_off - 1
+                    block = wide[start : start + frame_rows]
+                    if col_off == 0:
+                        block = jnp.where(column > 0, block, 0.0)
+                    if col_off == 2:
+                        block = jnp.where(column < columns - 1, block, 0.0)
+                    taps_mat[
+                        row_off,
+                        frame_rows * frame : frame_rows * (frame + 1),
+                        channels * col_off : channels * (col_off + 1),
+                    ] = block.astype(jnp.bfloat16)
         total = jnp.zeros(out_ref.shape, jnp.float32)
-        for tap in range(taps):
-            low, place = tap // 9 * frame_rows, tap % 9 * channels
-            total += lax.dot_general(
-                patch_ref[low : low + rows, place : place + channels],
-                weight_ref[taps - 1 - tap if backward else tap],
-                (((1,), (1 if backward else 0,)), ((), ())),
-                preferred_element_type=jnp.float32,
-            )
+        for depth_off in range(3):
+            low = depth_off * frame_rows
+            for row_off in range(3):
+                tap = 9 * depth_off + 3 * row_off
+                if not backward:
+                    total += jnp.dot(
+                        taps_mat[row_off, low : low + rows, :],
+                        weight_ref[tap : tap + 3].reshape(3 * channels, channels),
+                        preferred_element_type=jnp.float32,
+                    )
+                    continue
+                for col_off in range(3):
+                    total += lax.dot_general(
+                        taps_mat[
+                            row_off, low : low + rows, channels * col_off : channels * (col_off + 1)
+                        ],
+                        weight_ref[taps - 1 - tap - col_off],
+                        (((1,), (1,)), ((), ())),
+                        preferred_element_type=jnp.float32,
+                    )
         out_ref[...] = total
 
     if both:
@@ -54,25 +79,20 @@
         run(False)
 
 
-def conv_dot(patch_mat, kernel, both):
+def conv_dot(padded, kernel, rows, columns, both):
     channels = kernel.shape[1]
-    rows = patch_mat.shape[0] * 3 // 5
+    frame_rows = rows // 3
     return pl.pallas_call(
-        functools.partial(conv_kernel, both),
+        functools.partial(conv_kernel, both, columns),
         out_shape=jax.ShapeDtypeStruct((rows, channels), jnp.float32),
         in_specs=[pl.BlockSpec(memory_space=pltpu.VMEM)] * 2,
         out_specs=pl.BlockSpec(memory_space=pltpu.VMEM),
+        scratch_shapes=[
+            pltpu.VMEM((16 + 5 * (frame_rows + 2 * columns), channels), jnp.float32),
+            pltpu.VMEM((3, 5 * frame_rows, 3 * channels), jnp.bfloat16),
+        ],
         compiler_params=pltpu.CompilerParams(vmem_limit_bytes=24 * 2**20),
-    )(patch_mat, kernel)
-
-
-def spatial_patches(stacked, height, columns):
-    pieces = [
-        stacked[:, row_off : row_off + height, col_off : col_off + columns]
-        for row_off in range(3)
-        for col_off in range(3)
-    ]
-    return jnp.concatenate(pieces, axis=-1).reshape(stacked.shape[0] * height * columns, -1)
+    )(padded, kernel)
 
 
 def gather_kernel(clips, tiles, own_ref, all_ref, send_sem, recv_sem, local_sem):
@@ -197,60 +217,53 @@
     col_count = cols_used[0]
     upper_tile = neighbours[0, 0, 0]
     lower_tile = neighbours[0, 0, 1]
-    row_ids = jnp.arange(height, dtype=jnp.int32)
-    col_ids = jnp.arange(columns, dtype=jnp.int32)
-    inside = (row_ids[:, None] < row_count) & (col_ids[None, :] < col_count)
-    inside_mask = inside[None, :, :, None]
+    rows = frame_count * height * columns
+    tall = (height + 2) * columns
+    ids = lax.broadcasted_iota(jnp.int32, (rows, 1), 0)
+    inside = (ids // columns % height < row_count) & (ids % columns < col_count)
     kernel = weights[0]
-    front_zero = jnp.zeros((2, height + 2, columns + 2, channels), jnp.bfloat16)
 
     def halo_block(field):
-        leading = field[:, 0]
-        trailing = lax.dynamic_index_in_dim(field, row_count - 1, axis=1, keepdims=False)
+        frames = field.reshape(frame_count, height * columns, channels)
+        leading = frames[:, :columns]
+        trailing = lax.dynamic_slice_in_dim(frames, (row_count - 1) * columns, columns, 1)
         both_rows = jnp.stack([leading, trailing], axis=1)
         gathered = lax.all_gather(both_rows[None], "tile", axis=0, tiled=True)
         upper = gathered[jnp.minimum(upper_tile, tile_count - 1), :, 1]
         bottom = gathered[jnp.minimum(lower_tile, tile_count - 1), :, 0]
         upper = jnp.where(upper_tile < tile_count, upper, jnp.zeros_like(upper))
         bottom = jnp.where(lower_tile < tile_count, bottom, jnp.zeros_like(bottom))
-        return pad_block(field, upper, bottom, row_count)
+        padded = jnp.concatenate([upper, frames, jnp.zeros_like(upper)], axis=1)
+        padded = lax.dynamic_update_slice_in_dim(padded, bottom, (row_count + 1) * columns, axis=1)
+        return padded.reshape(frame_count * tall, channels)
 
     def flat(field):
-        rows = field.reshape(-1, channels)
-        return jnp.pad(rows, ((0, frame_count * (height + 2) * columns - rows.shape[0]), (0, 0)))
+        return jnp.pad(field, ((0, frame_count * tall - rows), (0, 0)))
 
     axes = ("clip", "tile")
     is_encoder = section == 0
-    source = jnp.where(inside_mask, video[0, 0], 0).astype(jnp.bfloat16)
-    target = jnp.where(inside_mask, cotangent[0, 0], 0).astype(jnp.bfloat16)
+    source = jnp.where(inside, video.reshape(rows, channels), 0).astype(jnp.bfloat16)
+    target = jnp.where(inside, cotangent.reshape(rows, channels), 0).astype(jnp.bfloat16)
     active = jax.nn.silu(source.astype(jnp.float32)).astype(jnp.bfloat16)
     padded = halo_block(jnp.where(is_encoder, active, target))
-    early = jnp.where(is_encoder, flat(padded[:, :, 1:-1]), flat(target))
+    early = jnp.where(is_encoder, padded, flat(target))
     early_all = lax.all_gather(early, axes, axis=0)
-    stacked = jnp.where(
-        is_encoder,
-        jnp.concatenate([front_zero, padded], axis=0),
-        jnp.concatenate([padded, front_zero], axis=0),
-    )
-    mixed = conv_dot(spatial_patches(stacked, height, columns), kernel, True).reshape(target.shape)
-    hidden = jnp.where(inside_mask, source.astype(jnp.float32) + mixed, 0.0).astype(jnp.bfloat16)
+    mixed = conv_dot(padded, kernel, rows, columns, True)
+    hidden = jnp.where(inside, source.astype(jnp.float32) + mixed, 0.0).astype(jnp.bfloat16)
     latent = shifted(hidden, "segment", 1)
     wide = latent.astype(jnp.float32)
     own_grad = jnp.where(
-        inside_mask, target.astype(jnp.float32) + silu_grad(wide) * mixed, 0.0
+        inside, target.astype(jnp.float32) + silu_grad(wide) * mixed, 0.0
     ).astype(jnp.bfloat16)
     returned = shifted(own_grad, "segment", -1)
     padded_two = halo_block(jax.nn.silu(wide).astype(jnp.bfloat16))
-    late = jnp.where(is_encoder, flat(returned), flat(padded_two[:, :, 1:-1]))
+    late = jnp.where(is_encoder, flat(returned), padded_two)
     late_all = gather_all(late)
-    stacked = jnp.concatenate([front_zero, padded_two], axis=0)
-    second = conv_dot(spatial_patches(stacked, height, columns), kernel, False)
-    decoded = jnp.where(
-        inside_mask, wide + second.reshape(target.shape), 0.0
-    ).astype(jnp.bfloat16)
-    own_out = jnp.where(is_encoder, hidden, decoded)
+    second = conv_dot(padded_two, kernel, rows, columns, False)
+    decoded = jnp.where(inside, wide + second, 0.0).astype(jnp.bfloat16)
+    own_out = jnp.where(is_encoder, hidden, decoded).reshape(video.shape[2:])
     acts = jnp.where(is_encoder, early_all, late_all)
-    ups = jnp.where(is_encoder, late_all, early_all)[:, : frame_count * height * columns]
+    ups = jnp.where(is_encoder, late_all, early_all)[:, :rows]
     summed = own_entries(acts, ups, axes, frame_count, height, columns)
     return (own_out[None, None, None], summed[None])
 

time: 114 us -> 122 us (1.070)
  waiting for transfers between devices: 0.04 us -> 33.9 us
  local copies, waits for them, and re-layouts: 30.7 us -> 11.7 us
  Pallas kernels: 27.9 us -> 24.9 us
  other arithmetic: 11.7 us -> 9.12 us
    all_gather x1, waiting for transfers between devices: 0.02 us -> 32.6 us  [local(): early_all = lax.all_gather(early, axes, axis=0)]
    unnamed x33 -> x21, local copies, waits for them, and re-layouts: 16.1 us -> 3.51 us
    reshape x7 -> x4, local copies, waits for them, and re-layouts: 8.78 us -> 4.89 us  [the longest x2 2.45 us: local(): video.reshape(rows, channels)]
    pallas_call x1, Pallas kernels: 26.5 us -> 23.4 us  [gather_all(): pl.pallas_call(functools.partial(gather_kernel, clips, tiles), out_shape=...]
    select_n x5 -> x4, other arithmetic: 0.98 us -> 2.77 us  [the longest x1 1.03 us: local(): jnp.where(inside, cotangent.reshape(rows, channels), 0).astype(jnp.bfloat16)]
    broadcast_in_dim x1 -> x0, other arithmetic: 1.74 us -> none  [local(): return (own_out[None, None, None], summed[None])]
    concatenate x3 -> x1, local copies, waits for them, and re-layouts: 1.53 us -> 0.08 us  [halo_block(): padded = jnp.concatenate([upper, frames, jnp.zeros_like(upper)], axis=1)]
    ppermute x2, waiting for transfers between devices: 0.01 us -> 1.25 us  [shifted(): return lax.ppermute(block, axis, route)]
  transfers between devices with their start and end apart: 3 -> 3, of which waited for: 0 -> 2; matrix products, arithmetic and copies ran while one was open for 25% -> 3% of each run, Pallas kernels for 25% -> 19%
where the time goes in v4:
time: 122 us
  waiting for transfers between devices  33.9 us (28%)
  Pallas kernels  24.9 us (20%)
  between operations  18.3 us (15%)
  blocking collectives  17.9 us (15%)
  local copies, waits for them, and re-layouts  11.7 us (10%)
  other arithmetic  9.12 us (7%)
  starting transfers between devices  3.25 us (3%)
  matrix products  2.7 us (2%)
    all_gather x1, waiting for transfers between devices, local(): early_all = lax.all_gather(early, axes, axis=0)  32.6 us
    pallas_call x1, Pallas kernels, gather_all(): pl.pallas_call(functools.partial(gather_kernel, clips, tiles), out_shape=...  23.4 us
    all_gather x2, blocking collectives, halo_block(): gathered = lax.all_gather(both_rows[None], 'tile', axis=0, tiled=True)  17.9 us
    unnamed x21, local copies, waits for them, and re-layouts  3.51 us
    ppermute x2, starting transfers between devices, shifted(): return lax.ppermute(block, axis, route)  3.21 us
    dot_general x6, matrix products, own_entries(): lax.dot_general(acts[:, :count], moved[:, frame_count - count:], contract...  2.7 us
    reshape x2, local copies, waits for them, and re-layouts, local(): video.reshape(rows, channels)  2.45 us
    reshape x2, local copies, waits for them, and re-layouts, local(): cotangent.reshape(rows, channels)  2.45 us
  transfers between devices with their start and end apart: 3, of which 2 were waited for; matrix products, arithmetic and copies ran while one was open for 3% of the time, Pallas kernels for 19%

profile of v4, /device:TPU:0, one launch (start us, length us, event | category | flops | bytes accessed | tf_op | source)
XLA Modules:
  0.0 121.7 jit_solution(4542912600385049348)
XLA Ops:
  7.2 0.0 all-gather.5.cloned.1.call-start
  7.2 1.3 %fusion.50 = (s32[1,1,1]{2,1,0:T(1,128)}, s32[1,1,1]{2,1,0:T(1,128)}) fusion(s32[1,1,2]{2,1,0:T(1,128)} %param.9), kind=kLoop, calls=%fused_computation.101 | loop fusion | bytes 16 | tf_op jit(solution)/shard_map/slice | solution.py:219
  11.1 0.9 reshape.185
  12.0 1.5 %reshape.184 = bf16[144,256]{1,0:T(8,128)(2,1)} reshape(bf16[1,1,3,12,4,256]{5,4,3,2,1,0:T(4,128)(2,1)} %param.6) | data formatting | bytes 147456 | tf_op jit(solution)/shard_map/reshape | solution.py:245
  14.9 0.9 reshape.186
  15.8 0.1 fusion.36
  16.0 9.7 %all-gather = bf16[12,2,4,256]{3,2,1,0:T(4,128)(2,1)S(1)} all-gather(bf16[3,2,4,256]{3,2,1,0:T(4,128)(2,1)S(1)} %pad_maximum_fusion.1), channel_id=2, replica_groups=mesh['segment'=2,'clip'=4,'tile'=4] {'tile'}, dimensions={0}, use_global_device_ids=true | all-gather | bytes 61440 | tf_op jit(solution)/shard_map/all_gather | solution.py:231
  25.7 0.1 pad.30.clone
  25.8 0.1 maximum_maximum_fusion
  25.9 2.0 %copy-done = bf16[1,27,256,256]{3,2,1,0:T(8,128)(2,1)S(1)} copy-done((bf16[1,27,256,256]{3,2,1,0:T(8,128)(2,1)S(1)}, bf16[1,27,256,256]{3,2,1,0:T(8,128)(2,1)}, u32[]{:S(2)}) %copy-start) | copy-done | bytes 3538968
  28.0 0.7 shard_map.77
  28.7 0.7 copy-done.2
  29.4 0.7 select_convert_fusion
  30.1 1.9 %collective-permute-start = (bf16[144,256]{1,0:T(8,128)(2,1)}, bf16[144,256]{1,0:T(8,128)(2,1)}, u32[]{:S(2)}, u32[]{:S(2)}) collective-permute-start(bf16[144,256]{1,0:T(8,128)(2,1)} %select_convert_fusion), channel_id=1, source_target_pairs={{0,16},{1,17},{2,18},{3,19},{4,20},{5,21},{6,22},{7,23},{8,24},{9,... | collective-permute-start | bytes 221192 | tf_op jit(solution)/shard_map/ppermute | solution.py:16
  32.0 1.5 %reshape.190 = bf16[144,256]{1,0:T(8,128)(2,1)} reshape(bf16[1,1,3,12,4,256]{5,4,3,2,1,0:T(4,128)(2,1)} %param.7) | data formatting | bytes 147456 | tf_op jit(solution)/shard_map/reshape | solution.py:246
  33.6 1.7 %fusion.29 = (bf16[144,256]{1,0:T(8,128)(2,1)}, bf16[144,256]{1,0:T(8,128)(2,1)S(1)}) fusion(f32[144,256]{1,0:T(8,128)} %copy-done.2, bf16[144,256]{1,0:T(8,128)(2,1)} %collective-permute-done, pred[144]{0:T(512)(128)(4,1)S(1)} %compare_and_fusion.2, bf16[144,256]{1,0:T(8,128)(2,1)} %reshape.190), kind=kLoop, calls=%fused_computation.49 | loop fusion | flops 589824 | bytes 442512 | tf_op jit(solution)/shard_map/convert_element_type | solution.py:257
  35.3 8.2 %all-gather.1 = bf16[12,2,4,256]{3,2,1,0:T(4,128)(2,1)S(1)} all-gather(bf16[3,2,4,256]{3,2,1,0:T(4,128)(2,1)S(1)} %pad_maximum_fusion.2), channel_id=3, replica_groups=mesh['segment'=2,'clip'=4,'tile'=4] {'tile'}, dimensions={0}, use_global_device_ids=true | all-gather | bytes 61440 | tf_op jit(solution)/shard_map/all_gather | solution.py:231
  43.6 0.1 maximum_maximum_fusion.1
  43.7 0.7 shard_map.78
  44.4 0.2 copy-done.7
  44.6 1.0 broadcast_select_fusion.1
  45.7 0.7 pad_select_fusion.1
  46.5 1.3 %collective-permute-start.1 = (bf16[144,256]{1,0:T(8,128)(2,1)}, bf16[144,256]{1,0:T(8,128)(2,1)S(1)}, u32[]{:S(2)}, u32[]{:S(2)}) collective-permute-start(bf16[144,256]{1,0:T(8,128)(2,1)} %get-tuple-element.4), channel_id=1, source_target_pairs={{16,0},{17,1},{18,2},{19,3},{20,4},{21,5},{22,6},{23,7},{24,8},{25... | collective-permute-start | bytes 221192 | tf_op jit(solution)/shard_map/ppermute | solution.py:16
  47.8 0.1 dynamic-slice.1
  47.8 0.1 dynamic-slice
  47.9 0.7 broadcast_in_dim_reshape.3
  48.6 1.2 %collective-permute-done.1 = bf16[144,256]{1,0:T(8,128)(2,1)S(1)} collective-permute-done((bf16[144,256]{1,0:T(8,128)(2,1)}, bf16[144,256]{1,0:T(8,128)(2,1)S(1)}, u32[]{:S(2)}, u32[]{:S(2)}) %collective-permute-start.1) | collective-permute-done | bytes 73760 | tf_op jit(solution)/shard_map/ppermute | solution.py:16
  49.8 0.9 pad_select_fusion.own_ref
  50.7 23.4 %shard_map.79 = bf16[4,4,168,256]{3,2,1,0:T(8,128)(2,1)S(1)} custom-call(bf16[168,256]{1,0:T(8,128)(2,1)S(1)} %pad_select_fusion.own_ref), custom_call_target="tpu_custom_call" | custom-call | tf_op jit(solution)/shard_map/pallas_call | solution.py:154
  74.2 32.6 %all-gather.5.cloned.1.call-done = bf16[2688,256]{1,0:T(8,128)(2,1)} async-done(((bf16[168,256]{1,0:T(8,128)(2,1)}), bf16[2688,256]{1,0:T(8,128)(2,1)}) %all-gather.5.cloned.1.call-update) | async-done | bytes 1376272 | tf_op jit(solution)/shard_map/all_gather | solution.py:250
  106.8 1.6 %broadcast_select_fusion = bf16[16,168,256]{2,1,0:T(8,128)(2,1)S(1)} fusion(bf16[16,168,256]{2,1,0:T(8,128)(2,1)} %bitcast.100, pred[]{:T(512)S(6)} %eq.11, bf16[4,4,168,256]{3,2,1,0:T(8,128)(2,1)S(1)} %shard_map.79), kind=kLoop, calls=%fused_computation.8 | loop fusion | flops 688128 | bytes 4128769 | tf_op jit(solution)/shard_map/jit(_where)/select_n | solution.py:265
  108.4 0.2 copy-done.6
  108.5 0.1 slice_select_fusion
  108.7 1.3 %fusion.1 = (bf16[16,3,56,256]{3,2,0,1:T(8,128)(2,1)S(1)}, bf16[16,3,56,256]{3,2,0,1:T(8,128)(2,1)S(1)}) fusion(s32[]{:T(128)S(6)} %select_n.252, pred[56]{0:T(512)(128)(4,1)S(1)} %dynamic-slice.1, s32[]{:T(128)S(6)} %select_n.248, pred[56]{0:T(512)(128)(4,1)S(1)} %dynamic-slice, bf16[16,3,48,256]{3,2,1,0:T(8,128)(2,1)S(1)} %bitcast.102), kind=kLoop, calls=%fused_computation.3 | loop fusion | flops 1376256 | bytes 3932280 | tf_op jit(solution)/shard_map/jit(_where)/select_n | solution.py:187
  110.0 0.4 convolution_bitcast_fusion.2
  110.5 0.3 convolution_bitcast_fusion
  110.8 0.6 fusion.9
  111.4 0.4 convolution_bitcast_fusion.3
  111.8 0.3 convolution_bitcast_fusion.1
  112.2 0.6 fusion.6
  112.8 0.1 fusion.33
  112.8 0.2 copy.34
  113.0 0.1 fusion.35
  113.1 0.2 copy.33
  113.2 0.1 fusion.31
  113.3 0.2 copy.35
  113.4 0.4 pad_maximum_fusion
  113.8 1.1 broadcast_in_dim.69
  (28 shorter events, 0.2 us)
Async XLA Ops:
  7.2 99.6 %all-gather.5.cloned.1.call-start = ((), (), s32[]{:S(2)}) async-start(), calls=%async_computation | async-start | bytes 1462272 | tf_op jit(solution)/shard_map/all_gather | solution.py:250
  25.9 2.8 %copy-start.4 = (bf16[3,56,256]{2,1,0:T(8,128)(2,1)}, bf16[3,56,256]{2,1,0:T(8,128)(2,1)S(1)}, u32[]{:S(2)}) copy-start(bf16[3,56,256]{2,1,0:T(8,128)(2,1)S(1)} %bitcast_dynamic-update-slice_fusion.1) | copy-start | bytes 258052
  25.9 2.0 %copy-start = (bf16[1,27,256,256]{3,2,1,0:T(8,128)(2,1)S(1)}, bf16[1,27,256,256]{3,2,1,0:T(8,128)(2,1)}, u32[]{:S(2)}) copy-start(bf16[1,27,256,256]{3,2,1,0:T(8,128)(2,1)} %param.8) | copy-start | bytes 10616836
  28.0 1.4 %copy-start.8 = (bf16[144,256]{1,0:T(8,128)(2,1)S(1)}, bf16[144,256]{1,0:T(8,128)(2,1)}, u32[]{:S(2)}) copy-start(bf16[144,256]{1,0:T(8,128)(2,1)} %reshape.184) | copy-start | bytes 221188
  28.0 15.7 %copy-start.1 = (bf16[1,27,256,256]{3,2,1,0:T(8,128)(2,1)S(1)}, bf16[1,27,256,256]{3,2,1,0:T(8,128)(2,1)}, u32[]{:S(2)}) copy-start(bf16[1,27,256,256]{3,2,1,0:T(8,128)(2,1)} %param.8) | copy-start | bytes 10616836
  28.7 0.7 copy-start.2
  30.1 3.5 %collective-permute-start = (bf16[144,256]{1,0:T(8,128)(2,1)}, bf16[144,256]{1,0:T(8,128)(2,1)}, u32[]{:S(2)}, u32[]{:S(2)}) collective-permute-start(bf16[144,256]{1,0:T(8,128)(2,1)} %select_convert_fusion), channel_id=1, source_target_pairs={{0,16},{1,17},{2,18},{3,19},{4,20},{5,21},{6,22},{7,23},{8,24},{9,... | collective-permute-start | bytes 221192 | tf_op jit(solution)/shard_map/ppermute | solution.py:16
  43.7 0.7 copy-start.3
  43.7 0.9 copy-start.7
  43.7 1.9 %copy-start.5 = (bf16[3,56,256]{2,1,0:T(8,128)(2,1)S(1)}, bf16[3,56,256]{2,1,0:T(8,128)(2,1)}, u32[]{:S(2)}) copy-start(bf16[3,56,256]{2,1,0:T(8,128)(2,1)} %copy-done.4) | copy-start | bytes 258052
  46.5 3.4 %collective-permute-start.1 = (bf16[144,256]{1,0:T(8,128)(2,1)}, bf16[144,256]{1,0:T(8,128)(2,1)S(1)}, u32[]{:S(2)}, u32[]{:S(2)}) collective-permute-start(bf16[144,256]{1,0:T(8,128)(2,1)} %get-tuple-element.4), channel_id=1, source_target_pairs={{16,0},{17,1},{18,2},{19,3},{20,4},{21,5},{22,6},{23,7},{24,8},{25... | collective-permute-start | bytes 221192 | tf_op jit(solution)/shard_map/ppermute | solution.py:16
  106.8 1.8 %copy-start.6 = (bf16[2688,256]{1,0:T(8,128)(2,1)S(1)}, bf16[2688,256]{1,0:T(8,128)(2,1)}, u32[]{:S(2)}) copy-start(bf16[2688,256]{1,0:T(8,128)(2,1)} %all-gather.5.cloned.1.call-done) | copy-start | bytes 4128772
Sparse Core Ops, SparseCore 0:
  46.5 60.2 all-gather.4

commit v5 on v4

--- a/solution.py
+++ b/solution.py
@@ -92,6 +92,7 @@
             pltpu.VMEM((3, 5 * frame_rows, 3 * channels), jnp.bfloat16),
         ],
         compiler_params=pltpu.CompilerParams(vmem_limit_bytes=24 * 2**20),
+        cost_estimate=pl.CostEstimate(flops=0, bytes_accessed=4096, transcendentals=0),
     )(padded, kernel)
 
 
@@ -164,6 +165,7 @@
         compiler_params=pltpu.CompilerParams(
             collective_id=0, has_side_effects=True, vmem_limit_bytes=32 * 2**20
         ),
+        cost_estimate=pl.CostEstimate(flops=0, bytes_accessed=4096, transcendentals=0),
     )(block)
     return gathered.reshape((clips * tiles,) + block.shape)
 
@@ -247,6 +249,7 @@
     active = jax.nn.silu(source.astype(jnp.float32)).astype(jnp.bfloat16)
     padded = halo_block(jnp.where(is_encoder, active, target))
     early = jnp.where(is_encoder, padded, flat(target))
+    early, padded = lax.optimization_barrier((early, padded))
     early_all = lax.all_gather(early, axes, axis=0)
     mixed = conv_dot(padded, kernel, rows, columns, True)
     hidden = jnp.where(inside, source.astype(jnp.float32) + mixed, 0.0).astype(jnp.bfloat16)

time: 122 us -> 102 us (0.84)
  waiting for transfers between devices: 33.9 us -> 12 us
  Pallas kernels: 24.9 us -> 27.2 us
    all_gather x1, waiting for transfers between devices: 32.6 us -> 11.5 us  [local(): early_all = lax.all_gather(early, axes, axis=0)]
    pallas_call x1, Pallas kernels: 23.4 us -> 25.9 us  [gather_all(): pl.pallas_call(functools.partial(gather_kernel, clips, tiles), out_shape=...]
    unnamed x21 -> x23, local copies, waits for them, and re-layouts: 3.51 us -> 4.19 us
  transfers between devices with their start and end apart: 3 -> 3, of which waited for: 2 -> 2; matrix products, arithmetic and copies ran while one was open for 3% -> 6% of each run, Pallas kernels for 19% -> 27%
where the time goes in v5:
time: 102 us; the launch traced here: 101 us
  Pallas kernels  27.2 us (27%)
  between operations  18.3 us (18%)
  blocking collectives  17.9 us (18%)
  waiting for transfers between devices  12 us (12%)
  local copies, waits for them, and re-layouts  10.9 us (11%)
  other arithmetic  9.24 us (9%)
  starting transfers between devices  3.23 us (3%)
  matrix products  2.7 us (3%)
    pallas_call x1, Pallas kernels, gather_all(): pl.pallas_call(functools.partial(gather_kernel, clips, tiles), out_shape=...  25.9 us
    all_gather x2, blocking collectives, halo_block(): gathered = lax.all_gather(both_rows[None], 'tile', axis=0, tiled=True)  17.9 us
    all_gather x1, waiting for transfers between devices, local(): early_all = lax.all_gather(early, axes, axis=0)  11.5 us
    unnamed x23, local copies, waits for them, and re-layouts  4.19 us
    ppermute x2, starting transfers between devices, shifted(): return lax.ppermute(block, axis, route)  3.19 us
    dot_general x6, matrix products, own_entries(): lax.dot_general(acts[:, :count], moved[:, frame_count - count:], contract...  2.7 us
  transfers between devices with their start and end apart: 3, of which 2 were waited for; matrix products, arithmetic and copies ran while one was open for 6% of the time, Pallas kernels for 27%

profile of v5, /device:TPU:0, one launch (start us, length us, event | category | flops | bytes accessed | tf_op | source)
XLA Modules:
  0.0 101.5 jit_solution(12770636008586402377)
XLA Ops:
  7.2 1.3 %fusion.50 = (s32[1,1,1]{2,1,0:T(1,128)}, s32[1,1,1]{2,1,0:T(1,128)}) fusion(s32[1,1,2]{2,1,0:T(1,128)} %param.9), kind=kLoop, calls=%fused_computation.101 | loop fusion | bytes 16 | tf_op jit(solution)/shard_map/slice | solution.py:221
  11.1 0.9 reshape.188
  12.1 0.9 reshape.186
  14.3 0.9 reshape.185
  15.2 0.1 fusion.36
  15.4 9.7 %all-gather = bf16[12,2,4,256]{3,2,1,0:T(4,128)(2,1)S(1)} all-gather(bf16[3,2,4,256]{3,2,1,0:T(4,128)(2,1)S(1)} %pad_maximum_fusion.1), channel_id=2, replica_groups=mesh['segment'=2,'clip'=4,'tile'=4] {'tile'}, dimensions={0}, use_global_device_ids=true | all-gather | bytes 61440 | tf_op jit(solution)/shard_map/all_gather | solution.py:233
  25.1 0.1 pad.30.clone
  25.2 0.1 broadcast_select_fusion.1
  25.4 0.1 maximum_maximum_fusion
  25.5 0.7 pad_select_fusion.1
  26.2 0.7 reshape.184
  26.8 2.0 %copy-done = bf16[1,27,256,256]{3,2,1,0:T(8,128)(2,1)S(1)} copy-done((bf16[1,27,256,256]{3,2,1,0:T(8,128)(2,1)S(1)}, bf16[1,27,256,256]{3,2,1,0:T(8,128)(2,1)}, u32[]{:S(2)}) %copy-start) | copy-done | bytes 3538968
  28.8 0.9 copy-done.5
  29.7 0.7 shard_map.77
  30.5 0.7 copy-done.2
  31.1 0.7 select_convert_fusion
  31.8 1.9 %collective-permute-start = (bf16[144,256]{1,0:T(8,128)(2,1)}, bf16[144,256]{1,0:T(8,128)(2,1)}, u32[]{:S(2)}, u32[]{:S(2)}) collective-permute-start(bf16[144,256]{1,0:T(8,128)(2,1)} %select_convert_fusion), channel_id=1, source_target_pairs={{0,16},{1,17},{2,18},{3,19},{4,20},{5,21},{6,22},{7,23},{8,24},{9,... | collective-permute-start | bytes 221192 | tf_op jit(solution)/shard_map/ppermute | solution.py:16
  33.8 0.1 dynamic-slice.1
  33.8 0.1 dynamic-slice
  33.9 0.4 collective-permute-done
  34.4 1.7 %fusion.29 = (bf16[144,256]{1,0:T(8,128)(2,1)}, bf16[144,256]{1,0:T(8,128)(2,1)S(1)}) fusion(f32[144,256]{1,0:T(8,128)} %copy-done.2, bf16[144,256]{1,0:T(8,128)(2,1)} %collective-permute-done, pred[144]{0:T(512)(128)(4,1)S(1)} %compare_and_fusion.2, bf16[144,256]{1,0:T(8,128)(2,1)} %copy-done.7), kind=kLoop, calls=%fused_computation.49 | loop fusion | flops 589824 | bytes 442512 | tf_op jit(solution)/shard_map/convert_element_type | solution.py:260
  36.1 1.3 %collective-permute-start.1 = (bf16[144,256]{1,0:T(8,128)(2,1)}, bf16[144,256]{1,0:T(8,128)(2,1)}, u32[]{:S(2)}, u32[]{:S(2)}) collective-permute-start(bf16[144,256]{1,0:T(8,128)(2,1)} %get-tuple-element.8), channel_id=1, source_target_pairs={{16,0},{17,1},{18,2},{19,3},{20,4},{21,5},{22,6},{23,7},{24,8},{25... | collective-permute-start | bytes 221192 | tf_op jit(solution)/shard_map/ppermute | solution.py:16
  37.4 8.2 %all-gather.1 = bf16[12,2,4,256]{3,2,1,0:T(4,128)(2,1)S(1)} all-gather(bf16[3,2,4,256]{3,2,1,0:T(4,128)(2,1)S(1)} %pad_maximum_fusion.2), channel_id=3, replica_groups=mesh['segment'=2,'clip'=4,'tile'=4] {'tile'}, dimensions={0}, use_global_device_ids=true | all-gather | bytes 61440 | tf_op jit(solution)/shard_map/all_gather | solution.py:233
  45.6 0.1 maximum_maximum_fusion.1
  45.8 0.7 shard_map.78
  46.5 1.0 %fusion.37 = bf16[144,256]{1,0:T(8,128)(2,1)S(1)} fusion(bf16[144,256]{1,0:T(8,128)(2,1)} %select_convert_fusion, f32[144,256]{1,0:T(8,128)S(1)} %shard_map.78, bf16[144,256]{1,0:T(8,128)(2,1)} %collective-permute-done, pred[144]{0:T(512)(128)(4,1)S(1)} %compare_and_fusion.2, pred[]{:T(512)S(6)} %eq.11), kind=kLoop, calls=%fused_computation.62 | loop fusion | flops 184320 | bytes 368785 | tf_op jit(solution)/shard_map/jit(_where)/select_n | solution.py:267
  47.5 0.7 broadcast_in_dim_reshape.3
  48.2 0.9 pad_select_fusion.own_ref
  49.1 25.9 %shard_map.79 = bf16[4,4,168,256]{3,2,1,0:T(8,128)(2,1)S(1)} custom-call(bf16[168,256]{1,0:T(8,128)(2,1)S(1)} %pad_select_fusion.own_ref), custom_call_target="tpu_custom_call" | custom-call | bytes 4096 | tf_op jit(solution)/shard_map/pallas_call | solution.py:155
  75.0 11.5 %all-gather.5.cloned.1.call-done = bf16[2688,256]{1,0:T(8,128)(2,1)} async-done(((bf16[168,256]{1,0:T(8,128)(2,1)}), bf16[2688,256]{1,0:T(8,128)(2,1)}) %all-gather.5.cloned.1.call-update) | async-done | bytes 1376272 | tf_op jit(solution)/shard_map/all_gather | solution.py:253
  86.5 1.6 %broadcast_select_fusion = bf16[16,168,256]{2,1,0:T(8,128)(2,1)S(1)} fusion(bf16[16,168,256]{2,1,0:T(8,128)(2,1)} %bitcast.100, pred[]{:T(512)S(6)} %eq.11, bf16[4,4,168,256]{3,2,1,0:T(8,128)(2,1)S(1)} %shard_map.79), kind=kLoop, calls=%fused_computation.8 | loop fusion | flops 688128 | bytes 4128769 | tf_op jit(solution)/shard_map/jit(_where)/select_n | solution.py:268
  88.1 0.2 copy-done.6
  88.3 0.1 slice_select_fusion
  88.4 1.3 %fusion.1 = (bf16[16,3,56,256]{3,2,0,1:T(8,128)(2,1)S(1)}, bf16[16,3,56,256]{3,2,0,1:T(8,128)(2,1)S(1)}) fusion(s32[]{:T(128)S(6)} %select_n.252, pred[56]{0:T(512)(128)(4,1)S(1)} %dynamic-slice.1, s32[]{:T(128)S(6)} %select_n.248, pred[56]{0:T(512)(128)(4,1)S(1)} %dynamic-slice, bf16[16,3,48,256]{3,2,1,0:T(8,128)(2,1)S(1)} %bitcast.102), kind=kLoop, calls=%fused_computation.3 | loop fusion | flops 1376256 | bytes 3932280 | tf_op jit(solution)/shard_map/jit(_where)/select_n | solution.py:189
  89.7 0.4 convolution_bitcast_fusion.2
  90.2 0.3 convolution_bitcast_fusion
  90.5 0.6 fusion.9
  91.1 0.4 convolution_bitcast_fusion.3
  91.6 0.3 convolution_bitcast_fusion.1
  91.9 0.6 fusion.6
  92.5 0.1 fusion.33
  92.5 0.2 copy.34
  92.7 0.1 fusion.35
  92.8 0.2 copy.33
  92.9 0.1 fusion.31
  93.0 0.2 copy.35
  93.1 0.4 pad_maximum_fusion
  93.5 1.1 %broadcast_in_dim.69 = f32[1,3,36864]{2,0,1:T(1,128)} reshape(f32[3,36864]{1,0:T(4,128)S(1)} %pad_maximum_fusion) | data formatting | bytes 884736 | tf_op jit(solution)/shard_map/broadcast_in_dim | solution.py:271
  (31 shorter events, 0.3 us)
Async XLA Ops:
  7.2 19.0 %copy-start.8 = (bf16[1,1,3,12,4,256]{5,4,3,2,1,0:T(4,128)(2,1)S(1)}, bf16[1,1,3,12,4,256]{5,4,3,2,1,0:T(4,128)(2,1)}, u32[]{:S(2)}) copy-start(bf16[1,1,3,12,4,256]{5,4,3,2,1,0:T(4,128)(2,1)} %param.6) | copy-start | bytes 221188
  7.2 79.3 %all-gather.5.cloned.1.call-start = ((), (), s32[]{:S(2)}) async-start(), calls=%async_computation | async-start | bytes 1462272 | tf_op jit(solution)/shard_map/all_gather | solution.py:253
  12.0 13.3 %copy-start.7 = (bf16[144,256]{1,0:T(8,128)(2,1)}, bf16[144,256]{1,0:T(8,128)(2,1)S(1)}, u32[]{:S(2)}) copy-start(bf16[144,256]{1,0:T(8,128)(2,1)S(1)} %reshape.188) | copy-start | bytes 221188
  25.5 1.4 %copy-start.4 = (bf16[3,56,256]{2,1,0:T(8,128)(2,1)}, bf16[3,56,256]{2,1,0:T(8,128)(2,1)S(1)}, u32[]{:S(2)}) copy-start(bf16[3,56,256]{2,1,0:T(8,128)(2,1)S(1)} %bitcast_dynamic-update-slice_fusion.1) | copy-start | bytes 258052
  26.8 2.0 %copy-start = (bf16[1,27,256,256]{3,2,1,0:T(8,128)(2,1)S(1)}, bf16[1,27,256,256]{3,2,1,0:T(8,128)(2,1)}, u32[]{:S(2)}) copy-start(bf16[1,27,256,256]{3,2,1,0:T(8,128)(2,1)} %param.8) | copy-start | bytes 10616836
  28.8 0.9 copy-start.5
  29.7 1.4 %copy-start.9 = (bf16[144,256]{1,0:T(8,128)(2,1)S(1)}, bf16[144,256]{1,0:T(8,128)(2,1)}, u32[]{:S(2)}) copy-start(bf16[144,256]{1,0:T(8,128)(2,1)} %reshape.184) | copy-start | bytes 221188
  29.7 16.0 %copy-start.1 = (bf16[1,27,256,256]{3,2,1,0:T(8,128)(2,1)S(1)}, bf16[1,27,256,256]{3,2,1,0:T(8,128)(2,1)}, u32[]{:S(2)}) copy-start(bf16[1,27,256,256]{3,2,1,0:T(8,128)(2,1)} %param.8) | copy-start | bytes 10616836
  30.4 0.7 copy-start.2
  31.8 2.5 %collective-permute-start = (bf16[144,256]{1,0:T(8,128)(2,1)}, bf16[144,256]{1,0:T(8,128)(2,1)}, u32[]{:S(2)}, u32[]{:S(2)}) collective-permute-start(bf16[144,256]{1,0:T(8,128)(2,1)} %select_convert_fusion), channel_id=1, source_target_pairs={{0,16},{1,17},{2,18},{3,19},{4,20},{5,21},{6,22},{7,23},{8,24},{9,... | collective-permute-start | bytes 221192 | tf_op jit(solution)/shard_map/ppermute | solution.py:16
  36.1 12.1 %collective-permute-start.1 = (bf16[144,256]{1,0:T(8,128)(2,1)}, bf16[144,256]{1,0:T(8,128)(2,1)}, u32[]{:S(2)}, u32[]{:S(2)}) collective-permute-start(bf16[144,256]{1,0:T(8,128)(2,1)} %get-tuple-element.8), channel_id=1, source_target_pairs={{16,0},{17,1},{18,2},{19,3},{20,4},{21,5},{22,6},{23,7},{24,8},{25... | collective-permute-start | bytes 221192 | tf_op jit(solution)/shard_map/ppermute | solution.py:16
  45.8 0.7 copy-start.3
  86.5 1.8 %copy-start.6 = (bf16[2688,256]{1,0:T(8,128)(2,1)S(1)}, bf16[2688,256]{1,0:T(8,128)(2,1)}, u32[]{:S(2)}) copy-start(bf16[2688,256]{1,0:T(8,128)(2,1)} %all-gather.5.cloned.1.call-done) | copy-start | bytes 4128772
Sparse Core Ops, SparseCore 0:
  26.3 60.1 all-gather.4

commit v6 on v5

--- a/solution.py
+++ b/solution.py
@@ -250,7 +250,9 @@
     padded = halo_block(jnp.where(is_encoder, active, target))
     early = jnp.where(is_encoder, padded, flat(target))
     early, padded = lax.optimization_barrier((early, padded))
-    early_all = lax.all_gather(early, axes, axis=0)
+    early_all = lax.all_gather(early, "tile", axis=0)
+    early_all = lax.all_gather(early_all, "clip", axis=0)
+    early_all = early_all.reshape((-1,) + early.shape)
     mixed = conv_dot(padded, kernel, rows, columns, True)
     hidden = jnp.where(inside, source.astype(jnp.float32) + mixed, 0.0).astype(jnp.bfloat16)
     latent = shifted(hidden, "segment", 1)

time: 102 us -> 104 us (1.020)
  the two profiles are of different devices: /device:TPU:0 before, /device:TPU:8 now
where the time goes in v6:
time: 104 us
  Pallas kernels  33 us (32%)
  blocking collectives  26.1 us (25%)
  between operations  18.3 us (18%)
  local copies, waits for them, and re-layouts  11.4 us (11%)
  other arithmetic  8.34 us (8%)
  starting transfers between devices  3.23 us (3%)
  matrix products  2.7 us (3%)
    pallas_call x1, Pallas kernels, gather_all(): pl.pallas_call(functools.partial(gather_kernel, clips, tiles), out_shape=...  31.6 us
    all_gather x2, blocking collectives, halo_block(): gathered = lax.all_gather(both_rows[None], 'tile', axis=0, tiled=True)  16 us
    all_gather x1, blocking collectives, local(): early_all = lax.all_gather(early, 'tile', axis=0)  10.1 us
    unnamed x21, local copies, waits for them, and re-layouts  4.66 us
    ppermute x2, starting transfers between devices, shifted(): return lax.ppermute(block, axis, route)  3.19 us
    dot_general x6, matrix products, own_entries(): lax.dot_general(acts[:, :count], moved[:, frame_count - count:], contract...  2.7 us
  transfers between devices with their start and end apart: 3, of which 1 were waited for; matrix products, arithmetic and copies ran while one was open for 6% of the time, Pallas kernels for 32%

profile of v6, /device:TPU:8, one launch (start us, length us, event | category | flops | bytes accessed | tf_op | source)
XLA Modules:
  0.0 103.5 jit_solution(275609778028360692)
XLA Ops:
  7.2 0.0 all-gather.6.cloned.1.call-start
  7.2 1.3 %fusion.50 = (s32[1,1,1]{2,1,0:T(1,128)}, s32[1,1,1]{2,1,0:T(1,128)}) fusion(s32[1,1,2]{2,1,0:T(1,128)} %param.9), kind=kLoop, calls=%fused_computation.101 | loop fusion | bytes 16 | tf_op jit(solution)/shard_map/slice | solution.py:221
  11.1 0.9 reshape.191
  12.1 0.9 reshape.189
  14.3 0.9 reshape.188
  15.2 0.1 fusion.36
  15.4 8.2 %all-gather = bf16[12,2,4,256]{3,2,1,0:T(4,128)(2,1)S(1)} all-gather(bf16[3,2,4,256]{3,2,1,0:T(4,128)(2,1)S(1)} %pad_maximum_fusion.1), channel_id=2, replica_groups=mesh['segment'=2,'clip'=4,'tile'=4] {'tile'}, dimensions={0}, use_global_device_ids=true | all-gather | bytes 61440 | tf_op jit(solution)/shard_map/all_gather | solution.py:233
  23.7 0.1 pad.30.clone
  23.8 0.1 broadcast_select_fusion.2
  23.9 0.1 maximum_maximum_fusion
  24.1 0.6 copy-done.4
  24.7 10.1 %all-gather.2 = bf16[672,256]{1,0:T(8,128)(2,1)} all-gather(bf16[168,256]{1,0:T(8,128)(2,1)S(1)} %pad_select_fusion.1), channel_id=4, replica_groups=mesh['segment'=2,'clip'=4,'tile'=4] {'tile'}, dimensions={0}, use_global_device_ids=true | all-gather | bytes 430080 | tf_op jit(solution)/shard_map/all_gather | solution.py:253
  34.8 0.7 reshape.187
  35.5 2.0 %copy-done = bf16[1,27,256,256]{3,2,1,0:T(8,128)(2,1)S(1)} copy-done((bf16[1,27,256,256]{3,2,1,0:T(8,128)(2,1)S(1)}, bf16[1,27,256,256]{3,2,1,0:T(8,128)(2,1)}, u32[]{:S(2)}) %copy-start) | copy-done | bytes 3538968
  37.5 0.9 copy-done.5
  38.4 0.7 shard_map.77
  39.1 0.7 copy-done.2
  39.7 0.7 select_convert_fusion
  40.5 1.9 %collective-permute-start = (bf16[144,256]{1,0:T(8,128)(2,1)}, bf16[144,256]{1,0:T(8,128)(2,1)}, u32[]{:S(2)}, u32[]{:S(2)}) collective-permute-start(bf16[144,256]{1,0:T(8,128)(2,1)} %select_convert_fusion), channel_id=1, source_target_pairs={{0,16},{1,17},{2,18},{3,19},{4,20},{5,21},{6,22},{7,23},{8,24},{9,... | collective-permute-start | bytes 221192 | tf_op jit(solution)/shard_map/ppermute | solution.py:16
  42.4 0.1 dynamic-slice.1
  42.5 0.1 dynamic-slice
  42.5 0.4 collective-permute-done
  43.0 1.7 %fusion.29 = (bf16[144,256]{1,0:T(8,128)(2,1)}, bf16[144,256]{1,0:T(8,128)(2,1)S(1)}) fusion(f32[144,256]{1,0:T(8,128)} %copy-done.2, bf16[144,256]{1,0:T(8,128)(2,1)} %collective-permute-done, pred[144]{0:T(512)(128)(4,1)S(1)} %compare_and_fusion.2, bf16[144,256]{1,0:T(8,128)(2,1)} %copy-done.6), kind=kLoop, calls=%fused_computation.49 | loop fusion | flops 589824 | bytes 442512 | tf_op jit(solution)/shard_map/convert_element_type | solution.py:262
  44.7 1.3 %collective-permute-start.1 = (bf16[144,256]{1,0:T(8,128)(2,1)}, bf16[144,256]{1,0:T(8,128)(2,1)}, u32[]{:S(2)}, u32[]{:S(2)}) collective-permute-start(bf16[144,256]{1,0:T(8,128)(2,1)} %get-tuple-element.10), channel_id=1, source_target_pairs={{16,0},{17,1},{18,2},{19,3},{20,4},{21,5},{22,6},{23,7},{24,8},{25... | collective-permute-start | bytes 221192 | tf_op jit(solution)/shard_map/ppermute | solution.py:16
  46.0 7.7 %all-gather.1 = bf16[12,2,4,256]{3,2,1,0:T(4,128)(2,1)S(1)} all-gather(bf16[3,2,4,256]{3,2,1,0:T(4,128)(2,1)S(1)} %pad_maximum_fusion.2), channel_id=3, replica_groups=mesh['segment'=2,'clip'=4,'tile'=4] {'tile'}, dimensions={0}, use_global_device_ids=true | all-gather | bytes 61440 | tf_op jit(solution)/shard_map/all_gather | solution.py:233
  53.8 0.1 maximum_maximum_fusion.1
  53.9 0.7 shard_map.78
  54.6 1.0 fusion.37
  55.6 0.7 broadcast_in_dim_reshape.3
  56.3 0.9 pad_select_fusion.own_ref
  57.2 31.6 %shard_map.79 = bf16[4,4,168,256]{3,2,1,0:T(8,128)(2,1)S(1)} custom-call(bf16[168,256]{1,0:T(8,128)(2,1)S(1)} %pad_select_fusion.own_ref), custom_call_target="tpu_custom_call" | custom-call | bytes 4096 | tf_op jit(solution)/shard_map/pallas_call | solution.py:155
  88.9 1.5 %broadcast_select_fusion = (bf16[4,4,168,256]{3,2,1,0:T(8,128)(2,1)S(1)}, bf16[4,4,168,256]{3,2,1,0:T(8,128)(2,1)S(1)}) fusion(bf16[4,4,168,256]{3,2,1,0:T(8,128)(2,1)S(1)} %shard_map.79, bf16[4,4,168,256]{3,2,1,0:T(8,128)(2,1)} %bitcast.101, pred[]{:T(512)S(6)} %eq.11), kind=kLoop, calls=%fused_computation.8 | loop fusion | flops 1376256 | bytes 5505025 | tf_op jit(solution)/shard_map/jit(_where)/select_n | solution.py:271
  90.4 0.1 slice.49
  90.5 1.3 %fusion.1 = (bf16[16,3,56,256]{3,2,0,1:T(8,128)(2,1)S(1)}, bf16[16,3,56,256]{3,2,0,1:T(8,128)(2,1)S(1)}) fusion(s32[]{:T(128)S(6)} %select_n.261, pred[56]{0:T(512)(128)(4,1)S(1)} %dynamic-slice.1, s32[]{:T(128)S(6)} %select_n.257, pred[56]{0:T(512)(128)(4,1)S(1)} %dynamic-slice, bf16[16,3,48,256]{3,2,1,0:T(8,128)(2,1)S(1)} %bitcast.100), kind=kLoop, calls=%fused_computation.3 | loop fusion | flops 1376256 | bytes 3932280 | tf_op jit(solution)/shard_map/jit(_where)/select_n | solution.py:189
  91.8 0.4 convolution_bitcast_fusion.2
  92.3 0.3 convolution_bitcast_fusion
  92.6 0.6 fusion.9
  93.2 0.4 convolution_bitcast_fusion.3
  93.6 0.3 convolution_bitcast_fusion.1
  94.0 0.6 fusion.6
  94.6 0.1 fusion.33
  94.6 0.2 copy.31
  94.8 0.1 fusion.35
  94.9 0.2 copy.30
  95.0 0.1 fusion.31
  95.1 0.2 copy.32
  95.2 0.4 pad_maximum_fusion
  95.6 1.1 %broadcast_in_dim.69 = f32[1,3,36864]{2,0,1:T(1,128)} reshape(f32[3,36864]{1,0:T(4,128)S(1)} %pad_maximum_fusion) | data formatting | bytes 884736 | tf_op jit(solution)/shard_map/broadcast_in_dim | solution.py:273
  (30 shorter events, 0.3 us)
Async XLA Ops:
  7.2 27.6 %copy-start.7 = (bf16[1,1,3,12,4,256]{5,4,3,2,1,0:T(4,128)(2,1)S(1)}, bf16[1,1,3,12,4,256]{5,4,3,2,1,0:T(4,128)(2,1)}, u32[]{:S(2)}) copy-start(bf16[1,1,3,12,4,256]{5,4,3,2,1,0:T(4,128)(2,1)} %param.6) | copy-start | bytes 221188
  7.2 81.7 %all-gather.6.cloned.1.call-start = ((), (), s32[]{:S(2)}) async-start(), calls=%async_computation | async-start | bytes 1720320 | tf_op jit(solution)/shard_map/all_gather | solution.py:254
  12.0 23.4 %copy-start.6 = (bf16[144,256]{1,0:T(8,128)(2,1)}, bf16[144,256]{1,0:T(8,128)(2,1)S(1)}, u32[]{:S(2)}) copy-start(bf16[144,256]{1,0:T(8,128)(2,1)S(1)} %reshape.191) | copy-start | bytes 221188
  24.0 0.6 copy-start.4
  35.5 2.0 %copy-start = (bf16[1,27,256,256]{3,2,1,0:T(8,128)(2,1)S(1)}, bf16[1,27,256,256]{3,2,1,0:T(8,128)(2,1)}, u32[]{:S(2)}) copy-start(bf16[1,27,256,256]{3,2,1,0:T(8,128)(2,1)} %param.8) | copy-start | bytes 10616836
  37.5 0.9 copy-start.5
  38.4 1.4 %copy-start.8 = (bf16[144,256]{1,0:T(8,128)(2,1)S(1)}, bf16[144,256]{1,0:T(8,128)(2,1)}, u32[]{:S(2)}) copy-start(bf16[144,256]{1,0:T(8,128)(2,1)} %reshape.187) | copy-start | bytes 221188
  38.4 15.5 %copy-start.1 = (bf16[1,27,256,256]{3,2,1,0:T(8,128)(2,1)S(1)}, bf16[1,27,256,256]{3,2,1,0:T(8,128)(2,1)}, u32[]{:S(2)}) copy-start(bf16[1,27,256,256]{3,2,1,0:T(8,128)(2,1)} %param.8) | copy-start | bytes 10616836
  39.1 0.7 copy-start.2
  40.5 2.5 %collective-permute-start = (bf16[144,256]{1,0:T(8,128)(2,1)}, bf16[144,256]{1,0:T(8,128)(2,1)}, u32[]{:S(2)}, u32[]{:S(2)}) collective-permute-start(bf16[144,256]{1,0:T(8,128)(2,1)} %select_convert_fusion), channel_id=1, source_target_pairs={{0,16},{1,17},{2,18},{3,19},{4,20},{5,21},{6,22},{7,23},{8,24},{9,... | collective-permute-start | bytes 221192 | tf_op jit(solution)/shard_map/ppermute | solution.py:16
  44.7 11.6 %collective-permute-start.1 = (bf16[144,256]{1,0:T(8,128)(2,1)}, bf16[144,256]{1,0:T(8,128)(2,1)}, u32[]{:S(2)}, u32[]{:S(2)}) collective-permute-start(bf16[144,256]{1,0:T(8,128)(2,1)} %get-tuple-element.10), channel_id=1, source_target_pairs={{16,0},{17,1},{18,2},{19,3},{20,4},{21,5},{22,6},{23,7},{24,8},{25... | collective-permute-start | bytes 221192 | tf_op jit(solution)/shard_map/ppermute | solution.py:16
  53.9 0.7 copy-start.3
Sparse Core Ops, SparseCore 0:
  34.9 38.3 all-gather.5
